TPU v7x, 32 devices: a whole 2x2x4 slice. The times are simulated.
32 devices in a mesh: seq: 16 (over z, y, core), fsdp: 2 (over x).
Axes of the slice: x: 2, y: 2, z: 4, core: 2. Of those that a mesh axis runs over, the one named last changes fastest.
Arguments:
- tokens: float32 [2, 2048, 768], P('fsdp', 'seq'), may hold values from -36 to 36
- cotangent: float32 [2, 2048, 768], P('fsdp', 'seq'), may hold values from -6 to 6
- qkv_weight: bfloat16 [2, 768, 2304], P(None, ('seq', 'fsdp')), may hold values from -0.21875 to 0.21875
- out_weight: bfloat16 [2, 768, 768], P(None, ('seq', 'fsdp')), may hold values from -2.5 to 2.5
- up_weight: bfloat16 [2, 768, 2304], P(None, ('seq', 'fsdp')), may hold values from -0.21875 to 0.21875
- down_weight: bfloat16 [2, 768, 1152], P(None, ('seq', 'fsdp')), may hold values from -0.1875 to 0.1875
- attn_gain: bfloat16 [2, 768], P(None, ('seq', 'fsdp')), may hold values from 0.5 to 1.5
- mlp_gain: bfloat16 [2, 768], P(None, ('seq', 'fsdp')), may hold values from 0.5 to 1.5
Outputs:
- stream_out: float32 [2, 2048, 768], P('fsdp', 'seq')
- grad_tokens: float32 [2, 2048, 768], P('fsdp', 'seq')
- qkv_grad: float32 [2, 768, 2304], P(None, ('seq', 'fsdp'))
- out_grad: float32 [2, 768, 768], P(None, ('seq', 'fsdp'))
- up_grad: float32 [2, 768, 2304], P(None, ('seq', 'fsdp'))
- down_grad: float32 [2, 768, 1152], P(None, ('seq', 'fsdp'))
- attn_gain_grad: float32 [2, 768], P(None, ('seq', 'fsdp'))
- mlp_gain_grad: float32 [2, 768], P(None, ('seq', 'fsdp'))
All inputs are finite; a program needn't handle non-finite values.
Results may differ from a plain program's by a relative error of at most 0.019.
Values may be sent and summed in bfloat16 or wider, within the bound.
No kernel may reach another device: no remote copies, remote signals or barrier semaphores. Data moves between devices by JAX's collectives and lax.ppermute only.
A program may use at most 256 MiB of HBM per device.

v0:
```python
import math

import jax
import jax.numpy as jnp
from jax import lax
from jax.sharding import PartitionSpec as P

D = 768
H = 12
HD = 64
FF = 1152
HALF = 64
LAYERS = 2


norm_eps = 1e-05
rope_base = 10000.0
inv_root_two = 1.0 / math.sqrt(2.0)
inv_root_tau = 1.0 / math.sqrt(2.0 * math.pi)


def with_halo(cells, sides, width):
    for axis, dim in sides:
        count = lax.axis_size(axis)
        ends = count - 1
        head = lax.slice_in_dim(cells, 0, width, axis=dim)
        tail = lax.slice_in_dim(cells, cells.shape[dim] - width, cells.shape[dim], axis=dim)
        cells = jnp.concatenate(
            [
                lax.ppermute(tail, axis, [(i, (i + 1) % count) for i in range(ends)]),
                cells,
                lax.ppermute(head, axis, [((i + 1) % count, i) for i in range(ends)]),
            ],
            axis=dim,
        )
    return cells


def layer_norm(values, norm_gain):
    center = values - jnp.mean(values, axis=-1, keepdims=True)
    inv_scale = lax.rsqrt(jnp.mean(center * center, axis=-1, keepdims=True) + norm_eps)
    normed = center * inv_scale
    return (normed, inv_scale, normed * norm_gain.astype(jnp.float32))


def norm_back(grad_out, normed, inv_scale, norm_gain):
    grad_hat = grad_out * norm_gain.astype(jnp.float32)
    mean_one = jnp.mean(grad_hat, axis=-1, keepdims=True)
    mean_two = jnp.mean(grad_hat * normed, axis=-1, keepdims=True)
    return inv_scale * (grad_hat - mean_one - normed * mean_two)


def gelu_value(values):
    return 0.5 * values * (1.0 + lax.erf(values * inv_root_two))


def gelu_slope(values):
    return 0.5 * (1.0 + lax.erf(values * inv_root_two)) + values * inv_root_tau * jnp.exp(
        -0.5 * values * values
    )


def rope_tables(positions, head_size):
    frequency = rope_base ** (-jnp.arange(0, head_size, 2).astype(jnp.float32) / head_size)
    angles = positions[:, None] * frequency[None, :]
    cosine = jnp.cos(angles)
    sine_part = jnp.sin(angles)
    return (
        jnp.concatenate([cosine, cosine], axis=-1)[:, None, :],
        jnp.concatenate([sine_part, sine_part], axis=-1)[:, None, :],
    )


def rotate_half(values):
    half_size = values.shape[-1] // 2
    return jnp.concatenate([-values[..., half_size:], values[..., :half_size]], axis=-1)


def rotate_back(values):
    half_size = values.shape[-1] // 2
    return jnp.concatenate([values[..., half_size:], -values[..., :half_size]], axis=-1)


def band_mask(query_count, halo_width, key_valid):
    query_pos = jnp.arange(query_count)[:, None]
    key_index = jnp.arange(query_count + 2 * halo_width)[None, :]
    offset = key_index - query_pos
    inside = (offset >= 0) & (offset <= 2 * halo_width)
    return inside[None, None, :, :] & key_valid[:, None, None, :]


def dot_rows(left_side, right_side):
    return lax.dot_general(
        left_side, right_side, (((0,), (0,)), ((), ())), preferred_element_type=jnp.float32
    )


def dot_cols(left_side, right_side):
    return lax.dot_general(
        left_side, right_side, (((1,), (1,)), ((), ())), preferred_element_type=jnp.float32
    )


def attend_forward(query_b, key_win, value_win, window_mask, score_scale):
    scores = (
        jnp.einsum("bqhe,bkhe->bhqk", query_b, key_win, preferred_element_type=jnp.float32)
        * score_scale
    )
    scores = jnp.where(window_mask, scores, -jnp.inf)
    log_total = jnp.log(jnp.sum(jnp.exp(scores), axis=-1))
    probs_b = jnp.exp(scores - log_total[..., None]).astype(jnp.bfloat16)
    attended = jnp.einsum("bhqk,bkhe->bqhe", probs_b, value_win, preferred_element_type=jnp.float32)
    return (attended.astype(jnp.bfloat16), log_total)


def attend_backward(
    query_b, key_win, value_win, window_mask, log_total, grad_attended, score_scale
):
    scores = (
        jnp.einsum("bqhe,bkhe->bhqk", query_b, key_win, preferred_element_type=jnp.float32)
        * score_scale
    )
    scores = jnp.where(window_mask, scores, -jnp.inf)
    attn_probs = jnp.exp(scores - log_total[..., None])
    probs_b = attn_probs.astype(jnp.bfloat16)
    grad_value = jnp.einsum(
        "bhqk,bqhe->bkhe", probs_b, grad_attended, preferred_element_type=jnp.float32
    )
    grad_probs = jnp.einsum(
        "bqhe,bkhe->bhqk", grad_attended, value_win, preferred_element_type=jnp.float32
    )
    row_inner = jnp.sum(attn_probs * grad_probs, axis=-1, keepdims=True)
    grad_scores = (attn_probs * (grad_probs - row_inner) * score_scale).astype(jnp.bfloat16)
    grad_query = jnp.einsum(
        "bhqk,bkhe->bqhe", grad_scores, key_win, preferred_element_type=jnp.float32
    )
    grad_key = jnp.einsum(
        "bhqk,bqhe->bkhe", grad_scores, query_b, preferred_element_type=jnp.float32
    )
    return (grad_query, grad_key, grad_value)


def local(tokens, cotangent, qkv_weight, out_weight, up_weight, down_weight, attn_gain, mlp_gain):
    row_count = tokens.shape[1]
    seq_count = lax.axis_size("seq")
    shard_count = lax.axis_size("fsdp")
    first_row = lax.axis_index("seq") * row_count
    length = row_count * seq_count
    width_keys = row_count + 2 * HALF
    score_scale = 1.0 / math.sqrt(HD)
    grad_factor = 1.0 / math.sqrt(length * shard_count)
    positions = (first_row + jnp.arange(row_count)).astype(jnp.float32)
    cosine_table, sine_table = rope_tables(positions, HD)
    key_pos = first_row - HALF + jnp.arange(width_keys)
    key_valid = ((key_pos >= 0) & (key_pos < length))[None, :]
    window_mask = band_mask(row_count, HALF, key_valid)
    stream = tokens.reshape(row_count, D)
    gains_one, qkv_all, out_all, gains_two, up_all, down_all = (
        lax.all_gather(attn_gain, ("seq", "fsdp"), axis=1, tiled=True),
        lax.all_gather(qkv_weight, ("seq", "fsdp"), axis=1, tiled=True),
        lax.all_gather(out_weight, ("seq", "fsdp"), axis=1, tiled=True),
        lax.all_gather(mlp_gain, ("seq", "fsdp"), axis=1, tiled=True),
        lax.all_gather(up_weight, ("seq", "fsdp"), axis=1, tiled=True),
        lax.all_gather(down_weight, ("seq", "fsdp"), axis=1, tiled=True),
    )
    layer_store = []
    for layer_index in range(LAYERS):
        normed_one, scale_one, pre_one = layer_norm(stream, gains_one[layer_index])
        attn_in = pre_one.astype(jnp.bfloat16)
        projected = jnp.dot(attn_in, qkv_all[layer_index], preferred_element_type=jnp.float32)
        query_raw = projected[:, :D].reshape(row_count, H, HD)
        key_raw = projected[:, D : 2 * D].reshape(row_count, H, HD)
        query_b = (query_raw * cosine_table + rotate_half(query_raw) * sine_table).astype(
            jnp.bfloat16
        )
        key_b = (key_raw * cosine_table + rotate_half(key_raw) * sine_table).astype(jnp.bfloat16)
        value_b = projected[:, 2 * D :].astype(jnp.bfloat16)
        key_value = jnp.concatenate([key_b.reshape(row_count, D), value_b], axis=1)[None]
        padded = with_halo(key_value, (("seq", 1),), HALF)
        key_win = padded[:, :, :D].reshape(1, width_keys, H, HD)
        value_win = padded[:, :, D:].reshape(1, width_keys, H, HD)
        query_b = query_b.reshape(1, row_count, H, HD)
        attended, log_total = attend_forward(query_b, key_win, value_win, window_mask, score_scale)
        attended = attended.reshape(row_count, D)
        middle = stream + jnp.dot(
            attended, out_all[layer_index], preferred_element_type=jnp.float32
        )
        normed_two, scale_two, pre_two = layer_norm(middle, gains_two[layer_index])
        ffn_in = pre_two.astype(jnp.bfloat16)
        lifted = jnp.dot(ffn_in, up_all[layer_index], preferred_element_type=jnp.float32)
        gate_part = lifted[:, :FF]
        linear_part = lifted[:, FF:]
        hidden_b = (gelu_value(gate_part) * linear_part).astype(jnp.bfloat16)
        layer_store.append(
            (
                normed_one,
                scale_one,
                attn_in,
                query_b,
                key_win,
                value_win,
                log_total,
                attended,
                normed_two,
                scale_two,
                ffn_in,
                gate_part,
                linear_part,
                hidden_b,
            )
        )
        stream = middle + dot_cols(hidden_b, down_all[layer_index])
    back_one, back_qkv, back_out, back_two, back_up, back_down = (
        gains_one,
        qkv_all,
        out_all,
        gains_two,
        up_all,
        down_all,
    )
    grad_stream = cotangent.reshape(row_count, D)
    kept_terms = [None] * LAYERS
    for layer_index in reversed(range(LAYERS)):
        (
            normed_one,
            scale_one,
            attn_in,
            query_b,
            key_win,
            value_win,
            log_total,
            attended,
            normed_two,
            scale_two,
            ffn_in,
            gate_part,
            linear_part,
            hidden_b,
        ) = layer_store[layer_index]
        grad_b = grad_stream.astype(jnp.bfloat16)
        grad_hidden = jnp.dot(grad_b, back_down[layer_index], preferred_element_type=jnp.float32)
        grad_lifted = jnp.concatenate(
            [
                grad_hidden * linear_part * gelu_slope(gate_part),
                grad_hidden * gelu_value(gate_part),
            ],
            axis=1,
        ).astype(jnp.bfloat16)
        grad_ffn_in = dot_cols(grad_lifted, back_up[layer_index])
        gain_two_vec = jnp.sum(grad_ffn_in * normed_two, axis=0)
        grad_middle = grad_stream + norm_back(
            grad_ffn_in, normed_two, scale_two, back_two[layer_index]
        )
        grad_middle_b = grad_middle.astype(jnp.bfloat16)
        grad_attended = (
            dot_cols(grad_middle_b, back_out[layer_index])
            .astype(jnp.bfloat16)
            .reshape(1, row_count, H, HD)
        )
        grad_query, grad_key_win, grad_value_win = attend_backward(
            query_b, key_win, value_win, window_mask, log_total, grad_attended, score_scale
        )
        window_grads = jnp.concatenate(
            [grad_key_win.reshape(1, width_keys, D), grad_value_win.reshape(1, width_keys, D)],
            axis=2,
        )
        edge_grads = jnp.concatenate(
            [window_grads[:, :HALF], window_grads[:, HALF + row_count :]], axis=1
        )
        returned = with_halo(edge_grads.astype(jnp.bfloat16), (("seq", 1),), HALF).astype(
            edge_grads.dtype
        )
        filler = jnp.zeros((1, row_count - 2 * HALF, 2 * D), jnp.float32)
        own_grads = window_grads[:, HALF : HALF + row_count] + jnp.concatenate(
            [returned[:, :HALF], filler, returned[:, 3 * HALF :]], axis=1
        )
        own_grads = own_grads.reshape(row_count, 2 * D)
        grad_query = grad_query.reshape(row_count, H, HD)
        grad_key = own_grads[:, :D].reshape(row_count, H, HD)
        grad_query_pre = grad_query * cosine_table + rotate_back(grad_query * sine_table)
        grad_key_pre = grad_key * cosine_table + rotate_back(grad_key * sine_table)
        grad_projected = jnp.concatenate(
            [
                grad_query_pre.reshape(row_count, D),
                grad_key_pre.reshape(row_count, D),
                own_grads[:, D:],
            ],
            axis=1,
        ).astype(jnp.bfloat16)
        grad_attn_in = dot_cols(grad_projected, back_qkv[layer_index])
        gain_one_vec = jnp.sum(grad_attn_in * normed_one, axis=0)
        grad_stream = grad_middle + norm_back(
            grad_attn_in, normed_one, scale_one, back_one[layer_index]
        )
        kept_terms[layer_index] = (
            attn_in,
            grad_projected,
            attended,
            grad_middle_b,
            ffn_in,
            grad_lifted,
            grad_b,
            hidden_b,
            gain_one_vec,
            gain_two_vec,
        )
    blocks = []
    gain_cols = []
    for layer_index in range(LAYERS):
        (
            attn_in,
            grad_projected,
            attended,
            grad_middle_b,
            ffn_in,
            grad_lifted,
            grad_b,
            hidden_b,
            gain_one_vec,
            gain_two_vec,
        ) = kept_terms[layer_index]
        blocks.append(dot_rows(attn_in, grad_projected))
        blocks.append(dot_rows(attended, grad_middle_b))
        blocks.append(dot_rows(ffn_in, grad_lifted))
        blocks.append(dot_rows(grad_b, hidden_b))
        gain_cols.append(gain_one_vec)
        gain_cols.append(gain_two_vec)
    matrix_part, gain_part = lax.psum_scatter(
        (jnp.concatenate(blocks, axis=1), jnp.stack(gain_cols, axis=1)),
        ("seq", "fsdp"),
        scatter_dimension=0,
        tiled=True,
    )
    own_rows = matrix_part.shape[0]
    layer_width = 4 * D + 3 * FF
    per_layer = (
        jnp.transpose(matrix_part.reshape(own_rows, LAYERS, layer_width), (1, 0, 2)) * grad_factor
    )
    qkv_part = per_layer[:, :, : 3 * D]
    out_part = per_layer[:, :, 3 * D : 4 * D]
    up_part = per_layer[:, :, 4 * D : 4 * D + 2 * FF]
    down_part = per_layer[:, :, 4 * D + 2 * FF :]
    gain_layers = jnp.transpose(gain_part.reshape(own_rows, LAYERS, 2), (1, 2, 0)) * grad_factor
    return (
        stream.reshape(1, row_count, D),
        grad_stream.reshape(1, row_count, D),
        qkv_part,
        out_part,
        up_part,
        down_part,
        gain_layers[:, 0],
        gain_layers[:, 1],
    )


def solution(mesh):
    placed = (
        P("fsdp", "seq", None),
        P("fsdp", "seq", None),
        P(None, ("seq", "fsdp"), None),
        P(None, ("seq", "fsdp"), None),
        P(None, ("seq", "fsdp"), None),
        P(None, ("seq", "fsdp"), None),
        P(None, ("seq", "fsdp")),
        P(None, ("seq", "fsdp")),
    )
    return jax.shard_map(
        local,
        mesh=mesh,
        in_specs=placed,
        out_specs=(
            P("fsdp", "seq", None),
            P("fsdp", "seq", None),
            P(None, ("seq", "fsdp"), None),
            P(None, ("seq", "fsdp"), None),
            P(None, ("seq", "fsdp"), None),
            P(None, ("seq", "fsdp"), None),
            P(None, ("seq", "fsdp")),
            P(None, ("seq", "fsdp")),
        ),
        check_vma=False,
    )
```

profile of v0, /device:TPU:0, one launch (start us, length us, event | category | flops | bytes accessed | tf_op | source)
XLA Modules:
  0.0 812.5 jit_solution(10470633519374697770)
XLA Ops:
  10.0 70.6 %all-gather = bf16[32,24,2]{1,2,0:T(2,128)(2,1)S(1)} all-gather(bf16[1,24,2]{1,2,0:T(2,128)(2,1)} %bitcast.304), channel_id=1, replica_groups=mesh['seq'=16,'fsdp'=2] {'seq','fsdp'}, dimensions={0}, use_global_device_ids=true | all-gather | bytes 3168 | tf_op jit(solution)/shard_map/all_gather | solution.py:159
  80.7 63.7 %all-gather.1 = bf16[32,24,2]{1,2,0:T(2,128)(2,1)S(1)} all-gather(bf16[1,24,2]{1,2,0:T(2,128)(2,1)} %bitcast.305), channel_id=1, replica_groups=mesh['seq'=16,'fsdp'=2] {'seq','fsdp'}, dimensions={0}, use_global_device_ids=true | all-gather | bytes 3168 | tf_op jit(solution)/shard_map/all_gather | solution.py:162
  146.1 2.7 fusion.6
  157.6 1.8 fusion.166
  159.7 58.6 %all-gather.11.cloned.1.call-done = bf16[2,768,2304]{2,1,0:T(8,128)(2,1)} async-done(((bf16[2,24,2304]{2,1,0:T(8,128)(2,1)}), bf16[2,768,2304]{2,1,0:T(8,128)(2,1)}) %all-gather.11.cloned.1.call-update) | async-done | bytes 7077904 | tf_op jit(solution)/shard_map/all_gather | solution.py:163
  218.2 3.7 fusion.8
  221.9 58.2 %all-gather.13.cloned.1.call-done = bf16[2,768,1152]{2,1,0:T(8,128)(2,1)} async-done(((bf16[2,24,1152]{2,1,0:T(8,128)(2,1)}), bf16[2,768,1152]{2,1,0:T(8,128)(2,1)}) %all-gather.13.cloned.1.call-update) | async-done | bytes 3538960 | tf_op jit(solution)/shard_map/all_gather | solution.py:164
  280.1 2.6 fusion.167
  282.9 2.7 fusion.10
  287.5 1.7 fusion.14
  289.2 1.9 copy.86
  294.1 2.0 fusion.155
  298.4 2.2 collective-permute-start.2
  302.8 1.9 collective-permute-done.3
  309.0 1.7 fusion.13
  310.8 3.5 convolution_convert_fusion.2
  314.3 1.8 fusion.168
  316.4 2.8 fusion.12
  320.7 4.3 multiply_reduce_fusion.2
  326.4 1.7 copy.91
  328.1 3.7 fusion.84
  331.9 2.7 fusion.175
  334.5 4.6 fusion.32
  340.6 6.1 collective-permute-start.4
  348.5 1.9 collective-permute-done.5
  354.4 4.8 bitcast_multiply_fusion.5
  362.6 4.5 multiply_reduce_fusion.3
  369.1 1.9 multiply_reduce_fusion.4
  373.2 1.7 copy.92
  374.9 2.5 fusion.87
  377.4 2.8 fusion.176
  380.2 3.5 fusion.38
  383.9 7.4 collective-permute-start.6
  391.3 1.6 collective-permute-start.7
  393.1 1.8 collective-permute-done.7
  398.7 4.6 bitcast_multiply_fusion.4
  406.4 4.0 convolution_dynamic-update-slice_fusion.3
  410.5 1.9 convolution_dynamic-update-slice_fusion.6
  412.4 4.0 convolution_dynamic-update-slice_fusion.2
  416.5 2.5 convolution_dynamic-update-slice_fusion.4
  419.0 4.0 convolution_dynamic-update-slice_fusion.1
  423.0 1.9 convolution_dynamic-update-slice_fusion.5
  425.0 4.1 convolution_dynamic-update-slice_fusion
  429.1 2.5 fusion.4
  432.3 2.9 fusion.44
  435.3 3.4 multiply_reduce_fusion.5
  438.8 48.2 %all-reduce = f32[768,4]{0,1:T(4,128)S(1)} all-reduce(f32[768,4]{0,1:T(4,128)S(1)} %pad_maximum_fusion.22), channel_id=3, replica_groups=mesh['seq'=16,'fsdp'=2] {'seq','fsdp'}, use_global_device_ids=true, to_apply=%region_25.26.clone | all-reduce | flops 3072 | bytes 24576
  488.6 313.6 %reduce-scatter.3.cloned.1.call-done = f32[24,13056]{1,0:T(8,128)} async-done(((f32[768,13056]{1,0:T(8,128)}), f32[24,13056]{1,0:T(8,128)}) %reduce-scatter.3.cloned.1.call-update) | async-done | bytes 1253392 | tf_op jit(solution)/shard_map/reduce_scatter | solution.py:328
  (312 shorter events, 58.1 us)
Async XLA Ops:
  7.2 137.8 %copy-start = (f32[1,128,768]{2,1,0:T(8,128)S(1)}, f32[1,128,768]{2,1,0:T(8,128)}, u32[]{:S(2)}) copy-start(f32[1,128,768]{2,1,0:T(8,128)} %param.8) | copy-start | bytes 1179652
  7.2 138.9 %all-gather.7.cloned.1.call-start = ((), (), s32[]{:S(2)}) async-start(), calls=%async_computation.1 | async-start | bytes 7299072 | tf_op jit(solution)/shard_map/all_gather | solution.py:160
  7.9 149.7 %all-gather.9.cloned.1.call-start = ((), (), s32[]{:S(2)}) async-start(), calls=%async_computation.2 | async-start | bytes 2433024 | tf_op jit(solution)/shard_map/all_gather | solution.py:161
  8.7 209.6 %all-gather.11.cloned.1.call-start = ((), (), s32[]{:S(2)}) async-start(), calls=%async_computation.3 | async-start | bytes 7299072 | tf_op jit(solution)/shard_map/all_gather | solution.py:163
  9.4 270.7 %all-gather.13.cloned.1.call-start = ((), (), s32[]{:S(2)}) async-start(), calls=%async_computation.4 | async-start | bytes 3649536 | tf_op jit(solution)/shard_map/all_gather | solution.py:164
  10.0 792.2 %reduce-scatter.3.cloned.1.call-start = ((), (), s32[]{:S(2)}) async-start(), calls=%async_computation.5 | async-start | bytes 41361408 | tf_op jit(solution)/shard_map/reduce_scatter | solution.py:328
  144.8 7.5 copy-start.24
  144.8 7.5 copy-start.34
  145.2 3.6 copy-start.60
  145.4 3.4 copy-start.71
  149.6 3.4 collective-permute-start
  150.9 3.3 collective-permute-start.1
  154.5 3.1 copy-start.11
  159.5 62.5 %copy-start.63 = (f32[128]{0:T(128)}, f32[128]{0:T(128)S(1)}, u32[]{:S(2)}) copy-start(f32[128]{0:T(128)S(1)} %broadcast_multiply_fusion.13) | copy-start | bytes 1540
  159.7 62.3 %copy-start.74 = (f32[128]{0:T(128)}, f32[128]{0:T(128)S(1)}, u32[]{:S(2)}) copy-start(f32[128]{0:T(128)S(1)} %add_rsqrt_fusion.2) | copy-start | bytes 1540
  297.2 4.8 copy-start.26
  297.3 4.8 copy-start.35
  298.4 4.4 collective-permute-start.2
  300.5 4.2 collective-permute-start.3
  306.7 4.0 copy-start.13
  316.2 8.8 %copy-start.69 = (f32[128]{0:T(128)}, f32[128]{0:T(128)S(1)}, u32[]{:S(2)}) copy-start(f32[128]{0:T(128)S(1)} %broadcast_multiply_fusion.11) | copy-start | bytes 1540
  316.4 8.6 %copy-start.80 = (f32[128]{0:T(128)}, f32[128]{0:T(128)S(1)}, u32[]{:S(2)}) copy-start(f32[128]{0:T(128)S(1)} %add_rsqrt_fusion) | copy-start | bytes 1540
  316.4 3.2 copy-start.85
  320.7 4.3 copy-start.52
  320.7 4.3 copy-start.54
  320.7 4.5 copy-start.1
  340.6 7.8 collective-permute-start.4
  346.7 3.6 collective-permute-start.5
  360.4 6.9 copy-start.86
  361.7 7.3 slice-start
  362.6 6.5 slice-start.1
  377.4 6.3 copy-start.15
  383.7 9.4 %copy-start.18 = (f32[12,64,256]{2,1,0:T(8,128)}, f32[12,64,256]{2,1,0:T(8,128)S(1)}, u32[]{:S(2)}) copy-start(f32[12,64,256]{2,1,0:T(8,128)S(1)} %fusion.38) | copy-start | bytes 2359300
  383.9 9.2 %collective-permute-start.6 = (bf16[1,64,1536]{1,2,0:T(8,128)(2,1)S(1)}, bf16[1,64,1536]{1,2,0:T(8,128)(2,1)S(1)}, u32[]{:S(2)}, u32[]{:S(2)}) collective-permute-start(bf16[1,64,1536]{1,2,0:T(8,128)(2,1)S(1)} %get-tuple-element.30), channel_id=1, source_target_pairs={{0,2},{2,4},{4,6},{6,8},{8,10},{10,12},{12,14},{14,16},{16,18},{18... | collective-permute-start | bytes 589832 | tf_op jit(solution)/shard_map/ppermute | solution.py:30
  391.3 3.6 collective-permute-start.7
  405.6 4.8 copy-start.48
  405.6 4.8 copy-start.50
  406.4 4.0 copy-start.5
  406.4 4.0 copy-start.38
  412.4 4.0 copy-start.10
  412.4 4.0 copy-start.21
  418.9 4.1 copy-start.39
  424.9 4.1 copy-start.23
  424.9 4.1 copy-start.29
  432.3 3.0 copy-start.43
  432.3 3.0 copy-start.49
  432.3 3.0 copy-start.51
  432.3 3.0 copy-start.62
  (54 other events, 99.6 us)
Sparse Core Ops, SparseCore 0:
  10.9 74.8 all-gather.6
  88.6 55.9 all-gather.8
  147.5 70.6 all-gather.10
  221.0 59.0 all-gather.12
  431.7 370.4 reduce-scatter.2
where the time goes:
time: 814 us; the launch traced here: 813 us
  waiting for transfers between devices  440 us (54%)
  blocking collectives  183 us (22%)
  matrix products  101 us (12%)
  local copies, waits for them, and re-layouts  27.7 us (3%)
  other arithmetic  23.6 us (3%)
  starting transfers between devices  23 us (3%)
  between operations  15.3 us (2%)
    reduce_scatter x1, waiting for transfers between devices, local(): lax.psum_scatter((jnp.concatenate(blocks, axis=1), jnp.stack(gain_cols, a...  314 us
    all_gather x1, blocking collectives, local(): lax.all_gather(attn_gain, ('seq', 'fsdp'), axis=1, tiled=True)  70.6 us
    all_gather x1, blocking collectives, local(): lax.all_gather(mlp_gain, ('seq', 'fsdp'), axis=1, tiled=True)  63.7 us
    all_gather x1, waiting for transfers between devices, local(): lax.all_gather(up_weight, ('seq', 'fsdp'), axis=1, tiled=True)  58.6 us
    all_gather x1, waiting for transfers between devices, local(): lax.all_gather(down_weight, ('seq', 'fsdp'), axis=1, tiled=True)  58.2 us
    unnamed x1, blocking collectives  48.2 us
    dot_general x8, matrix products, dot_rows(): lax.dot_general(left_side, right_side, (((0,), (0,)), ((), ())), preferre...  25 us
    dot_general x8, matrix products, dot_cols(): lax.dot_general(left_side, right_side, (((1,), (1,)), ((), ())), preferre...  22 us
  transfers between devices with their start and end apart: 13, of which 7 were waited for; matrix products, arithmetic and copies ran while one was open for 3% of the time, Pallas kernels for 0%

commit v1 on v0

--- a/solution.py
+++ b/solution.py
@@ -11,6 +11,7 @@
 FF = 1152
 HALF = 64
 LAYERS = 2
+LANES = 128
 
 
 norm_eps = 1e-05
@@ -138,6 +139,34 @@
         "bhqk,bqhe->bkhe", grad_scores, query_b, preferred_element_type=jnp.float32
     )
     return (grad_query, grad_key, grad_value)
+
+
+def gather_layer(qkv, out, up, down, gain_one, gain_two):
+    rows = qkv.shape[0]
+    gains = jnp.pad(jnp.stack([gain_one, gain_two], axis=1), ((0, 0), (0, LANES - 2)))
+    packed = jnp.concatenate([qkv, out, up, down, gains], axis=1)
+    whole = lax.all_gather(packed, ("seq", "fsdp"), axis=0, tiled=True)
+    first = 0
+    parts = []
+    for width in (qkv.shape[1], out.shape[1], up.shape[1], down.shape[1], LANES):
+        parts.append(whole[:, first : first + width])
+        first += width
+    return (parts[4][:, 0], parts[0], parts[1], parts[4][:, 1], parts[2], parts[3])
+
+
+def scatter_layer(blocks, gain_vecs, grad_factor):
+    gains = jnp.pad(jnp.stack(gain_vecs, axis=1), ((0, 0), (0, LANES - 2)))
+    packed = jnp.concatenate(
+        [part.astype(jnp.bfloat16) for part in (*blocks, gains)], axis=1
+    )
+    own = lax.psum_scatter(packed, ("seq", "fsdp"), scatter_dimension=0, tiled=True)
+    own = own.astype(jnp.float32) * grad_factor
+    first = 0
+    parts = []
+    for part in blocks:
+        parts.append(own[:, first : first + part.shape[1]])
+        first += part.shape[1]
+    return (*parts, own[:, first], own[:, first + 1])
 
 
 def local(tokens, cotangent, qkv_weight, out_weight, up_weight, down_weight, attn_gain, mlp_gain):
@@ -155,13 +184,13 @@
     key_valid = ((key_pos >= 0) & (key_pos < length))[None, :]
     window_mask = band_mask(row_count, HALF, key_valid)
     stream = tokens.reshape(row_count, D)
-    gains_one, qkv_all, out_all, gains_two, up_all, down_all = (
-        lax.all_gather(attn_gain, ("seq", "fsdp"), axis=1, tiled=True),
-        lax.all_gather(qkv_weight, ("seq", "fsdp"), axis=1, tiled=True),
-        lax.all_gather(out_weight, ("seq", "fsdp"), axis=1, tiled=True),
-        lax.all_gather(mlp_gain, ("seq", "fsdp"), axis=1, tiled=True),
-        lax.all_gather(up_weight, ("seq", "fsdp"), axis=1, tiled=True),
-        lax.all_gather(down_weight, ("seq", "fsdp"), axis=1, tiled=True),
+    gains_one, qkv_all, out_all, gains_two, up_all, down_all = zip(
+        *(
+            gather_layer(
+                qkv_weight[n], out_weight[n], up_weight[n], down_weight[n], attn_gain[n], mlp_gain[n]
+            )
+            for n in range(LAYERS)
+        )
     )
     layer_store = []
     for layer_index in range(LAYERS):
@@ -219,7 +248,7 @@
         down_all,
     )
     grad_stream = cotangent.reshape(row_count, D)
-    kept_terms = [None] * LAYERS
+    layer_grads = [None] * LAYERS
     for layer_index in reversed(range(LAYERS)):
         (
             normed_one,
@@ -292,55 +321,19 @@
         grad_stream = grad_middle + norm_back(
             grad_attn_in, normed_one, scale_one, back_one[layer_index]
         )
-        kept_terms[layer_index] = (
-            attn_in,
-            grad_projected,
-            attended,
-            grad_middle_b,
-            ffn_in,
-            grad_lifted,
-            grad_b,
-            hidden_b,
-            gain_one_vec,
-            gain_two_vec,
-        )
-    blocks = []
-    gain_cols = []
-    for layer_index in range(LAYERS):
-        (
-            attn_in,
-            grad_projected,
-            attended,
-            grad_middle_b,
-            ffn_in,
-            grad_lifted,
-            grad_b,
-            hidden_b,
-            gain_one_vec,
-            gain_two_vec,
-        ) = kept_terms[layer_index]
-        blocks.append(dot_rows(attn_in, grad_projected))
-        blocks.append(dot_rows(attended, grad_middle_b))
-        blocks.append(dot_rows(ffn_in, grad_lifted))
-        blocks.append(dot_rows(grad_b, hidden_b))
-        gain_cols.append(gain_one_vec)
-        gain_cols.append(gain_two_vec)
-    matrix_part, gain_part = lax.psum_scatter(
-        (jnp.concatenate(blocks, axis=1), jnp.stack(gain_cols, axis=1)),
-        ("seq", "fsdp"),
-        scatter_dimension=0,
-        tiled=True,
-    )
-    own_rows = matrix_part.shape[0]
-    layer_width = 4 * D + 3 * FF
-    per_layer = (
-        jnp.transpose(matrix_part.reshape(own_rows, LAYERS, layer_width), (1, 0, 2)) * grad_factor
-    )
-    qkv_part = per_layer[:, :, : 3 * D]
-    out_part = per_layer[:, :, 3 * D : 4 * D]
-    up_part = per_layer[:, :, 4 * D : 4 * D + 2 * FF]
-    down_part = per_layer[:, :, 4 * D + 2 * FF :]
-    gain_layers = jnp.transpose(gain_part.reshape(own_rows, LAYERS, 2), (1, 2, 0)) * grad_factor
+        layer_grads[layer_index] = scatter_layer(
+            (
+                dot_rows(attn_in, grad_projected),
+                dot_rows(attended, grad_middle_b),
+                dot_rows(ffn_in, grad_lifted),
+                dot_rows(grad_b, hidden_b),
+            ),
+            (gain_one_vec, gain_two_vec),
+            grad_factor,
+        )
+    qkv_part, out_part, up_part, down_part, gain_one_part, gain_two_part = map(
+        jnp.stack, zip(*layer_grads)
+    )
     return (
         stream.reshape(1, row_count, D),
         grad_stream.reshape(1, row_count, D),
@@ -348,8 +341,8 @@
         out_part,
         up_part,
         down_part,
-        gain_layers[:, 0],
-        gain_layers[:, 1],
+        gain_one_part,
+        gain_two_part,
     )
 
 

time: 814 us -> 602 us (0.74)
  blocking collectives: 183 us -> 0 us
  waiting for transfers between devices: 440 us -> 388 us
  local copies, waits for them, and re-layouts: 27.7 us -> 36.1 us
    all_gather x2 -> x0, blocking collectives: 134 us -> none  [the longest x1 70.6 us: local(): lax.all_gather(attn_gain, ('seq', 'fsdp'), axis=1, tiled=True)]
    reduce_scatter x1 -> x2, waiting for transfers between devices: 314 us -> 223 us  [scatter_layer(): lax.psum_scatter(packed, ('seq', 'fsdp'), scatter_dimension=0, tiled=True)]
    unnamed x1 -> x0, blocking collectives: 48.2 us -> none
    all_gather x4 -> x2, waiting for transfers between devices: 117 us -> 164 us  [gather_layer(): whole = lax.all_gather(packed, ('seq', 'fsdp'), axis=0, tiled=True)]
  transfers between devices with their start and end apart: 13 -> 12, of which waited for: 7 -> 6; matrix products, arithmetic and copies ran while one was open for 3% -> 10% of each run, Pallas kernels for 0% -> 0%
where the time goes in v1:
time: 602 us; the launch traced here: 600 us
  waiting for transfers between devices  388 us (64%)
  matrix products  102 us (17%)
  local copies, waits for them, and re-layouts  36.1 us (6%)
  other arithmetic  29.7 us (5%)
  starting transfers between devices  28.9 us (5%)
  between operations  15.3 us (3%)
    reduce_scatter x2, waiting for transfers between devices, scatter_layer(): lax.psum_scatter(packed, ('seq', 'fsdp'), scatter_dimension=0, tiled=True)  223 us
    all_gather x2, waiting for transfers between devices, gather_layer(): whole = lax.all_gather(packed, ('seq', 'fsdp'), axis=0, tiled=True)  164 us
    dot_general x8, matrix products, dot_cols(): lax.dot_general(left_side, right_side, (((1,), (1,)), ((), ())), preferre...  27.7 us
    ppermute x4, starting transfers between devices, with_halo(): lax.ppermute(tail, axis, [(i, (i + 1) % count) for i in range(ends)])  23.5 us
    dot_general x8, matrix products, dot_rows(): lax.dot_general(left_side, right_side, (((0,), (0,)), ((), ())), preferre...  20.1 us
    unnamed x174, local copies, waits for them, and re-layouts  12.8 us
  transfers between devices with their start and end apart: 12, of which 6 were waited for; matrix products, arithmetic and copies ran while one was open for 10% of the time, Pallas kernels for 0%

profile of v1, /device:TPU:0, one launch (start us, length us, event | category | flops | bytes accessed | tf_op | source)
XLA Modules:
  0.0 600.1 jit_solution(7107207536439319437)
XLA Ops:
  15.0 86.0 %all-gather.3.cloned.1.call-done = bf16[768,6656]{1,0:T(8,128)(2,1)} async-done(((bf16[24,6656]{1,0:T(8,128)(2,1)}), bf16[768,6656]{1,0:T(8,128)(2,1)}) %all-gather.3.cloned.1.call-update) | async-done | bytes 10223632 | tf_op jit(solution)/shard_map/all_gather | solution.py:148
  102.3 2.7 fusion.23
  107.0 3.0 collective-permute-start
  110.2 78.1 %all-gather.5.cloned.1.call-done = bf16[768,6656]{1,0:T(8,128)(2,1)} async-done(((bf16[24,6656]{1,0:T(8,128)(2,1)}), bf16[768,6656]{1,0:T(8,128)(2,1)}) %all-gather.5.cloned.1.call-update) | async-done | bytes 10223632 | tf_op jit(solution)/shard_map/all_gather | solution.py:148
  192.8 1.8 fusion.180
  194.8 2.7 fusion.19
  197.5 2.6 fusion.181
  200.4 2.7 fusion.15
  205.0 1.9 copy.92
  209.9 2.0 fusion.170
  214.0 3.7 collective-permute-start.2
  224.2 1.7 fusion.27
  225.9 3.3 convolution_convert_fusion.10
  229.2 1.8 fusion.182
  231.3 2.7 fusion.11
  234.0 2.5 fusion.95
  236.6 4.2 multiply_reduce_fusion.2
  241.0 2.5 convolution_convert_fusion.9
  243.6 1.8 copy.98
  245.3 2.8 fusion.191
  248.1 3.6 fusion.113
  251.7 4.5 fusion.49
  256.2 1.5 fusion.81
  259.0 4.9 collective-permute-start.4
  269.0 4.8 bitcast_multiply_fusion.5
  277.0 3.1 fusion.5
  280.1 1.6 fusion.60
  281.7 3.0 fusion.4
  284.7 2.0 fusion.26
  286.7 4.6 multiply_reduce_fusion.3
  293.4 1.7 pad_dynamic-update-slice_fusion
  295.2 1.7 fusion.28
  298.1 2.2 fusion.100
  300.4 4.1 multiply_reduce_fusion.4
  304.8 2.5 convolution_convert_fusion.8
  307.3 1.7 copy.99
  309.0 2.5 fusion.116
  311.6 2.6 fusion.192
  314.2 3.7 fusion.55
  319.5 11.9 %collective-permute-start.6 = (bf16[1,64,1536]{1,2,0:T(8,128)(2,1)S(1)}, bf16[1,64,1536]{1,2,0:T(8,128)(2,1)S(1)}, u32[]{:S(2)}, u32[]{:S(2)}) collective-permute-start(bf16[1,64,1536]{1,2,0:T(8,128)(2,1)S(1)} %get-tuple-element.34), channel_id=1, source_target_pairs={{0,2},{2,4},{4,6},{6,8},{8,10},{10,12},{12,14},{14,16},{16,18},{18... | collective-permute-start | bytes 589832 | tf_op jit(solution)/shard_map/ppermute | solution.py:31
  336.4 4.6 bitcast_multiply_fusion.4
  343.2 4.1 multiply_reduce_fusion.5
  347.5 4.0 fusion.7
  353.1 3.1 fusion.6
  356.2 1.9 fusion.8
  360.2 2.9 fusion.68
  364.0 79.3 %reduce-scatter.5.cloned.1.call-done = bf16[24,6656]{1,0:T(8,128)(2,1)} async-done(((bf16[768,6656]{1,0:T(8,128)(2,1)}), bf16[24,6656]{1,0:T(8,128)(2,1)}) %reduce-scatter.5.cloned.1.call-update) | async-done | bytes 319504 | tf_op jit(solution)/shard_map/reduce_scatter | solution.py:162
  444.6 143.5 %reduce-scatter.3.cloned.1.call-done = bf16[24,6656]{1,0:T(8,128)(2,1)} async-done(((bf16[768,6656]{1,0:T(8,128)(2,1)}), bf16[24,6656]{1,0:T(8,128)(2,1)}) %reduce-scatter.3.cloned.1.call-update) | async-done | bytes 319504 | tf_op jit(solution)/shard_map/reduce_scatter | solution.py:162
  (316 shorter events, 62.5 us)
Async XLA Ops:
  7.2 7.4 %copy-start = (f32[1,128,768]{2,1,0:T(8,128)S(1)}, f32[1,128,768]{2,1,0:T(8,128)}, u32[]{:S(2)}) copy-start(f32[1,128,768]{2,1,0:T(8,128)} %param.8) | copy-start | bytes 1179652
  7.2 93.8 %all-gather.3.cloned.1.call-start = ((), (), s32[]{:S(2)}) async-start(), calls=%async_computation.2 | async-start | bytes 10543104 | tf_op jit(solution)/shard_map/all_gather | solution.py:148
  13.2 175.1 %all-gather.5.cloned.1.call-start = ((), (), s32[]{:S(2)}) async-start(), calls=%async_computation.3 | async-start | bytes 10543104 | tf_op jit(solution)/shard_map/all_gather | solution.py:148
  14.1 429.2 %reduce-scatter.5.cloned.1.call-start = ((), (), s32[]{:S(2)}) async-start(), calls=%async_computation.5 | async-start | bytes 10543104 | tf_op jit(solution)/shard_map/reduce_scatter | solution.py:162
  14.4 175.2 %copy-start.31 = (f32[128,64]{0,1:T(8,128)}, f32[128,64]{0,1:T(8,128)S(1)}, u32[]{:S(2)}) copy-start(f32[128,64]{0,1:T(8,128)S(1)} %get-tuple-element.108) | copy-start | bytes 98308
  14.4 193.6 %copy-start.22 = (f32[128,64]{0,1:T(8,128)}, f32[128,64]{0,1:T(8,128)S(1)}, u32[]{:S(2)}) copy-start(f32[128,64]{0,1:T(8,128)S(1)} %get-tuple-element.109) | copy-start | bytes 98308
  14.7 90.3 %copy-start.64 = (f32[128]{0:T(128)}, f32[128]{0:T(128)S(1)}, u32[]{:S(2)}) copy-start(f32[128]{0:T(128)S(1)} %broadcast_multiply_fusion.13) | copy-start | bytes 1540
  14.9 90.1 %copy-start.71 = (f32[128]{0:T(128)}, f32[128]{0:T(128)S(1)}, u32[]{:S(2)}) copy-start(f32[128]{0:T(128)S(1)} %add_rsqrt_fusion.3) | copy-start | bytes 1540
  15.0 175.9 %copy-start.42 = (pred[128,256]{1,0:T(8,128)(4,1)}, pred[128,256]{1,0:T(8,128)(4,1)S(1)}, u32[]{:S(2)}) copy-start(pred[128,256]{1,0:T(8,128)(4,1)S(1)} %fusion.139) | copy-start | bytes 98308
  105.7 84.0 %collective-permute-start.1 = (bf16[1,64,1536]{2,1,0:T(8,128)(2,1)S(1)}, bf16[1,64,1536]{2,1,0:T(8,128)(2,1)S(1)}, u32[]{:S(2)}, u32[]{:S(2)}) collective-permute-start(bf16[1,64,1536]{2,1,0:T(8,128)(2,1)S(1)} %get-tuple-element.69), channel_id=1, source_target_pairs={{2,0},{4,2},{6,4},{8,6},{10,8},{12,10},{14,12},{16,14},{18,16},{20... | collective-permute-start | bytes 589832 | tf_op jit(solution)/shard_map/ppermute | solution.py:33
  107.0 82.7 %collective-permute-start = (bf16[1,64,1536]{2,1,0:T(8,128)(2,1)S(1)}, bf16[1,64,1536]{2,1,0:T(8,128)(2,1)S(1)}, u32[]{:S(2)}, u32[]{:S(2)}) collective-permute-start(bf16[1,64,1536]{2,1,0:T(8,128)(2,1)S(1)} %get-tuple-element.68), channel_id=1, source_target_pairs={{0,2},{2,4},{4,6},{6,8},{8,10},{10,12},{12,14},{14,16},{16,18},{18... | collective-permute-start | bytes 589832 | tf_op jit(solution)/shard_map/ppermute | solution.py:31
  192.8 4.7 copy-start.34
  194.6 2.9 copy-start.54
  200.2 2.9 copy-start.68
  212.7 7.7 %collective-permute-start.3 = (bf16[1,64,1536]{2,1,0:T(8,128)(2,1)}, bf16[1,64,1536]{2,1,0:T(8,128)(2,1)}, u32[]{:S(2)}, u32[]{:S(2)}) collective-permute-start(bf16[1,64,1536]{2,1,0:T(8,128)(2,1)} %get-tuple-element.63), channel_id=1, source_target_pairs={{2,0},{4,2},{6,4},{8,6},{10,8},{12,10},{14,12},{16,14},{18,16},{20... | collective-permute-start | bytes 589832 | tf_op jit(solution)/shard_map/ppermute | solution.py:33
  214.0 6.5 %collective-permute-start.2 = (bf16[1,64,1536]{2,1,0:T(8,128)(2,1)}, bf16[1,64,1536]{2,1,0:T(8,128)(2,1)}, u32[]{:S(2)}, u32[]{:S(2)}) collective-permute-start(bf16[1,64,1536]{2,1,0:T(8,128)(2,1)} %get-tuple-element.62), channel_id=1, source_target_pairs={{0,2},{2,4},{4,6},{6,8},{8,10},{10,12},{12,14},{14,16},{16,18},{18... | collective-permute-start | bytes 589832 | tf_op jit(solution)/shard_map/ppermute | solution.py:31
  222.7 3.2 copy-start.9
  231.0 9.8 %copy-start.56 = (f32[128]{0:T(128)}, f32[128]{0:T(128)S(1)}, u32[]{:S(2)}) copy-start(f32[128]{0:T(128)S(1)} %broadcast_multiply_fusion.10) | copy-start | bytes 1540
  231.3 9.6 %copy-start.62 = (f32[128]{0:T(128)}, f32[128]{0:T(128)S(1)}, u32[]{:S(2)}) copy-start(f32[128]{0:T(128)S(1)} %add_rsqrt_fusion) | copy-start | bytes 1540
  236.6 4.2 copy-start.47
  236.6 4.2 copy-start.49
  256.2 7.7 %copy-start.78 = (bf16[768]{0:T(1024)(128)(2,1)S(1)}, bf16[768]{0:T(1024)(128)(2,1)}, u32[]{:S(2)}) copy-start(bf16[768]{0:T(1024)(128)(2,1)} %get-tuple-element.18) | copy-start | bytes 4612
  257.7 7.0 %collective-permute-start.5 = (bf16[1,64,1536]{1,2,0:T(8,128)(2,1)S(1)}, bf16[1,64,1536]{1,2,0:T(8,128)(2,1)S(1)}, u32[]{:S(2)}, u32[]{:S(2)}) collective-permute-start(bf16[1,64,1536]{1,2,0:T(8,128)(2,1)S(1)} %get-tuple-element.39), channel_id=1, source_target_pairs={{2,0},{4,2},{6,4},{8,6},{10,8},{12,10},{14,12},{16,14},{18,16},{20... | collective-permute-start | bytes 589832 | tf_op jit(solution)/shard_map/ppermute | solution.py:33
  259.0 6.0 collective-permute-start.4
  277.0 3.1 copy-start.37
  281.7 3.0 copy-start.20
  281.7 3.0 copy-start.28
  286.7 4.6 copy-start.58
  295.1 293.1 %reduce-scatter.3.cloned.1.call-start = ((), (), s32[]{:S(2)}) async-start(), calls=%async_computation.4 | async-start | bytes 10543104 | tf_op jit(solution)/shard_map/reduce_scatter | solution.py:162
  298.1 6.4 %copy-start.5 = (f32[128,768]{1,0:T(8,128)}, f32[128,768]{1,0:T(8,128)S(1)}, u32[]{:S(2)}) copy-start(f32[128,768]{1,0:T(8,128)S(1)} %multiply_add_fusion.1) | copy-start | bytes 1179652
  300.3 4.2 copy-start.43
  300.4 4.2 copy-start.45
  304.7 6.8 %copy-start.25 = (bf16[1,256,768]{1,2,0:T(8,128)(2,1)S(1)}, bf16[1,256,768]{1,2,0:T(8,128)(2,1)}, u32[]{:S(2)}) copy-start(bf16[1,256,768]{1,2,0:T(8,128)(2,1)} %copy.87) | copy-start | bytes 1179652
  311.6 6.4 %copy-start.10 = (f32[12,64,256]{2,1,0:T(8,128)S(1)}, f32[12,64,256]{2,1,0:T(8,128)}, u32[]{:S(2)}) copy-start(f32[12,64,256]{2,1,0:T(8,128)} %fusion.116) | copy-start | bytes 2359300
  314.2 17.1 %copy-start.79 = (bf16[768]{0:T(1024)(128)(2,1)S(1)}, bf16[768]{0:T(1024)(128)(2,1)}, u32[]{:S(2)}) copy-start(bf16[768]{0:T(1024)(128)(2,1)} %get-tuple-element.14) | copy-start | bytes 4612
  317.9 13.7 %copy-start.14 = (f32[12,64,256]{2,1,0:T(8,128)}, f32[12,64,256]{2,1,0:T(8,128)S(1)}, u32[]{:S(2)}) copy-start(f32[12,64,256]{2,1,0:T(8,128)S(1)} %fusion.55) | copy-start | bytes 2359300
  318.2 13.5 %collective-permute-start.7 = (bf16[1,64,1536]{1,2,0:T(8,128)(2,1)S(1)}, bf16[1,64,1536]{1,2,0:T(8,128)(2,1)S(1)}, u32[]{:S(2)}, u32[]{:S(2)}) collective-permute-start(bf16[1,64,1536]{1,2,0:T(8,128)(2,1)S(1)} %get-tuple-element.35), channel_id=1, source_target_pairs={{2,0},{4,2},{6,4},{8,6},{10,8},{12,10},{14,12},{16,14},{18,16},{20... | collective-permute-start | bytes 589832 | tf_op jit(solution)/shard_map/ppermute | solution.py:33
  319.5 13.1 %collective-permute-start.6 = (bf16[1,64,1536]{1,2,0:T(8,128)(2,1)S(1)}, bf16[1,64,1536]{1,2,0:T(8,128)(2,1)S(1)}, u32[]{:S(2)}, u32[]{:S(2)}) collective-permute-start(bf16[1,64,1536]{1,2,0:T(8,128)(2,1)S(1)} %get-tuple-element.34), channel_id=1, source_target_pairs={{0,2},{2,4},{4,6},{6,8},{8,10},{10,12},{12,14},{14,16},{16,18},{18... | collective-permute-start | bytes 589832 | tf_op jit(solution)/shard_map/ppermute | solution.py:31
  342.4 4.9 copy-start.53
  343.1 4.3 copy-start.66
  343.2 4.3 copy-start.73
  347.5 4.0 copy-start.35
  353.0 3.1 copy-start.6
  353.0 3.1 copy-start.18
  360.1 2.9 copy-start.81
  360.1 2.9 copy-start.80
  360.2 2.9 copy-start.67
  360.2 2.9 copy-start.74
  (48 other events, 77.4 us)
Sparse Core Ops, SparseCore 0:
  13.3 87.6 all-gather.2
  104.5 83.7 all-gather.4
  295.2 148.1 reduce-scatter.4
  449.2 138.8 reduce-scatter.2

commit v2 on v1

v2 whole, which is shorter than its diff:
```python
import functools
import math

import jax
import jax.numpy as jnp
from jax import lax
from jax.experimental import pallas as pl
from jax.experimental.pallas import tpu as pltpu
from jax.sharding import PartitionSpec as P


D = 768
H = 12
HD = 64
FF = 1152
HALF = 64
LAYERS = 2
LANES = 128


norm_eps = 1e-05
rope_base = 10000.0
inv_root_two = 1.0 / math.sqrt(2.0)
inv_root_tau = 1.0 / math.sqrt(2.0 * math.pi)
score_scale = 1.0 / math.sqrt(HD)
bf16 = jnp.bfloat16
f32 = jnp.float32


def rope_tables(positions, head_size):
    frequency = rope_base ** (-jnp.arange(0, head_size, 2).astype(f32) / head_size)
    angles = positions[:, None] * frequency[None, :]
    cosine = jnp.cos(angles)
    sine_part = jnp.sin(angles)
    return jnp.tile(cosine, (1, 2 * H)), jnp.tile(sine_part, (1, 2 * H))


def dot_plain(left_side, right_side):
    return jnp.dot(left_side, right_side, preferred_element_type=f32)


def dot_rows(left_side, right_side):
    return lax.dot_general(
        left_side, right_side, (((0,), (0,)), ((), ())), preferred_element_type=f32
    )


def dot_cols(left_side, right_side):
    return lax.dot_general(
        left_side, right_side, (((1,), (1,)), ((), ())), preferred_element_type=f32
    )


def layer_norm(values, norm_gain):
    center = values - jnp.mean(values, axis=-1, keepdims=True)
    inv_scale = lax.rsqrt(jnp.mean(center * center, axis=-1, keepdims=True) + norm_eps)
    normed = center * inv_scale
    return (normed, inv_scale, normed * norm_gain)


def norm_back(grad_out, normed, inv_scale, norm_gain):
    grad_hat = grad_out * norm_gain
    mean_one = jnp.mean(grad_hat, axis=-1, keepdims=True)
    mean_two = jnp.mean(grad_hat * normed, axis=-1, keepdims=True)
    return inv_scale * (grad_hat - mean_one - normed * mean_two)


def half_rolls(values):
    width = values.shape[1]
    lane = lax.broadcasted_iota(jnp.int32, values.shape, 1) % HD
    ahead = pltpu.roll(values, width - HD // 2, 1)
    behind = pltpu.roll(values, HD // 2, 1)
    return lane < HD // 2, ahead, behind


def rotate(values, cosine, sine):
    low, ahead, behind = half_rolls(values)
    return values * cosine + jnp.where(low, -ahead, behind) * sine


def rotate_back(values, cosine, sine):
    low, ahead, behind = half_rolls(values * sine)
    return values * cosine + jnp.where(low, ahead, -behind)


def window_mask(first_row, row_count, length):
    shape = (row_count, row_count + 2 * HALF)
    key = lax.broadcasted_iota(jnp.int32, shape, 1)
    offset = key - lax.broadcasted_iota(jnp.int32, shape, 0)
    place = key + (first_row - HALF)
    return (offset >= 0) & (offset <= 2 * HALF) & (place >= 0) & (place < length)


def fill_window(window_ref, own_ref, before_ref, after_ref):
    rows = own_ref.shape[0]
    window_ref[:HALF] = before_ref[...]
    window_ref[HALF : HALF + rows] = own_ref[...]
    window_ref[HALF + rows :] = after_ref[...]


def pair_cols(ref, pair, base=0):
    return ref[:, base + pair * LANES : base + (pair + 1) * LANES]


def of_head(values, side):
    lane = lax.broadcasted_iota(jnp.int32, values.shape, 1)
    return jnp.where(lane // HD == side, values, jnp.zeros_like(values))


def project_kernel(stream_ref, gain_ref, weight_ref, cos_ref, sin_ref, *outs):
    normed_ref, scale_ref, input_ref, query_ref, keyval_ref = outs
    normed, scale, pre = layer_norm(stream_ref[...], gain_ref[...])
    attn_in = pre.astype(bf16)
    normed_ref[...] = normed
    scale_ref[...] = scale
    input_ref[...] = attn_in
    cosine, sine = cos_ref[...], sin_ref[...]
    query_ref[...] = rotate(dot_plain(attn_in, weight_ref[:, :D]), cosine, sine).astype(bf16)
    keys = dot_plain(attn_in, weight_ref[:, D : 2 * D])
    keyval_ref[:, :D] = rotate(keys, cosine, sine).astype(bf16)
    keyval_ref[:, D:] = dot_plain(attn_in, weight_ref[:, 2 * D :]).astype(bf16)


def forward_kernel(length, place_ref, query_ref, keyval_ref, before_ref, after_ref, stream_ref,
                   gain_ref, out_ref, up_ref, down_ref, *rest):
    attended_ref, total_ref, normed_ref, scale_ref, input_ref = rest[:5]
    gate_ref, linear_ref, hidden_ref, result_ref, window_ref = rest[5:]
    rows = query_ref.shape[0]
    fill_window(window_ref, keyval_ref, before_ref, after_ref)
    mask = window_mask(place_ref[0], rows, length)
    lane = lax.broadcasted_iota(jnp.int32, (rows, LANES), 1)
    totals = jnp.zeros((rows, LANES), f32)
    for pair in range(H // 2):
        query = pair_cols(query_ref, pair)
        keys = pair_cols(window_ref, pair)
        values = pair_cols(window_ref, pair, D)
        mixed = []
        for side in range(2):
            scores = dot_cols(of_head(query, side), keys) * score_scale
            scores = jnp.where(mask, scores, -jnp.inf)
            log_total = jnp.log(jnp.sum(jnp.exp(scores), axis=-1, keepdims=True))
            probs = jnp.exp(scores - log_total).astype(bf16)
            mixed.append(dot_plain(probs, values))
            totals = jnp.where(lane == 2 * pair + side, log_total, totals)
        attended_ref[:, pair * LANES : (pair + 1) * LANES] = jnp.where(
            lane // HD == 0, mixed[0], mixed[1]
        ).astype(bf16)
    total_ref[...] = totals
    middle = stream_ref[...] + dot_plain(attended_ref[...], out_ref[...])
    normed, scale, pre = layer_norm(middle, gain_ref[...])
    ffn_in = pre.astype(bf16)
    normed_ref[...] = normed
    scale_ref[...] = scale
    input_ref[...] = ffn_in
    gate = dot_plain(ffn_in, up_ref[:, :FF])
    linear = dot_plain(ffn_in, up_ref[:, FF:])
    gate_ref[...] = gate
    linear_ref[...] = linear
    hidden = (0.5 * gate * (1.0 + lax.erf(gate * inv_root_two)) * linear).astype(bf16)
    hidden_ref[...] = hidden
    result_ref[...] = middle + dot_cols(hidden, down_ref[...])


def backward_kernel(length, place_ref, grad_ref, normed_ref, scale_ref, gate_ref, linear_ref,
                    gain_ref, down_ref, up_ref, out_ref, query_ref, keyval_ref, before_ref,
                    after_ref, total_ref, cos_ref, sin_ref, *rest):
    rounded_ref, lifted_ref, middle_ref, middle_b_ref, gain_sum_ref = rest[:5]
    grad_query_ref, own_ref, to_before_ref, to_after_ref, window_ref, queries_ref = rest[5:]
    rows = query_ref.shape[0]
    grad = grad_ref[...]
    grad_b = grad.astype(bf16)
    rounded_ref[...] = grad_b
    grad_hidden = dot_plain(grad_b, down_ref[...])
    gate = gate_ref[...]
    curve = 0.5 * (1.0 + lax.erf(gate * inv_root_two))
    slope = curve + gate * inv_root_tau * jnp.exp(-0.5 * gate * gate)
    lifted_ref[:, :FF] = (grad_hidden * linear_ref[...] * slope).astype(bf16)
    lifted_ref[:, FF:] = (grad_hidden * (gate * curve)).astype(bf16)
    grad_in = dot_cols(lifted_ref[...], up_ref[...])
    normed = normed_ref[...]
    gain_sum_ref[...] = jnp.sum(grad_in * normed, axis=0, keepdims=True)
    grad_middle = grad + norm_back(grad_in, normed, scale_ref[...], gain_ref[...])
    middle_ref[...] = grad_middle
    grad_middle_b = grad_middle.astype(bf16)
    middle_b_ref[...] = grad_middle_b
    grad_attended = dot_cols(grad_middle_b, out_ref[...]).astype(bf16)
    fill_window(window_ref, keyval_ref, before_ref, after_ref)
    mask = window_mask(place_ref[0], rows, length)
    lane = lax.broadcasted_iota(jnp.int32, (rows, LANES), 1)
    for pair in range(H // 2):
        query = pair_cols(query_ref, pair)
        keys = pair_cols(window_ref, pair)
        values = pair_cols(window_ref, pair, D)
        grads = grad_attended[:, pair * LANES : (pair + 1) * LANES]
        grad_query = []
        grad_keys = jnp.zeros((rows + 2 * HALF, LANES), f32)
        grad_values = jnp.zeros((rows + 2 * HALF, LANES), f32)
        for side in range(2):
            head_query = of_head(query, side)
            head_grads = of_head(grads, side)
            scores = dot_cols(head_query, keys) * score_scale
            scores = jnp.where(mask, scores, -jnp.inf)
            head = 2 * pair + side
            probs = jnp.exp(scores - total_ref[:, head : head + 1])
            grad_values = grad_values + dot_rows(probs.astype(bf16), head_grads)
            grad_probs = dot_cols(head_grads, values)
            row_inner = jnp.sum(probs * grad_probs, axis=-1, keepdims=True)
            grad_scores = (probs * (grad_probs - row_inner) * score_scale).astype(bf16)
            grad_query.append(dot_plain(grad_scores, keys))
            grad_keys = grad_keys + dot_rows(grad_scores, head_query)
        cols = slice(pair * LANES, (pair + 1) * LANES)
        queries_ref[:, cols] = jnp.where(lane // HD == 0, grad_query[0], grad_query[1])
        for base, part in ((0, grad_keys), (D, grad_values)):
            cols = slice(base + pair * LANES, base + (pair + 1) * LANES)
            to_before_ref[:, cols] = part[:HALF].astype(bf16)
            own_ref[:, cols] = part[HALF : HALF + rows]
            to_after_ref[:, cols] = part[HALF + rows :].astype(bf16)
    grad_query_ref[...] = rotate_back(queries_ref[...], cos_ref[...], sin_ref[...]).astype(bf16)


def input_grad_kernel(grad_query_ref, own_ref, before_ref, after_ref, weight_ref, gain_ref,
                      normed_ref, scale_ref, middle_ref, cos_ref, sin_ref, *outs):
    projected_ref, result_ref, gain_sum_ref, total_ref = outs
    rows = own_ref.shape[0]
    total_ref[...] = own_ref[...]
    total_ref[:HALF] = total_ref[:HALF] + before_ref[...].astype(f32)
    total_ref[rows - HALF :] = total_ref[rows - HALF :] + after_ref[...].astype(f32)
    projected_ref[:, :D] = grad_query_ref[...]
    keys = rotate_back(total_ref[:, :D], cos_ref[...], sin_ref[...])
    projected_ref[:, D : 2 * D] = keys.astype(bf16)
    projected_ref[:, 2 * D :] = total_ref[:, D:].astype(bf16)
    grad_in = dot_cols(projected_ref[...], weight_ref[...])
    normed = normed_ref[...]
    gain_sum_ref[...] = jnp.sum(grad_in * normed, axis=0, keepdims=True)
    result_ref[...] = middle_ref[...] + norm_back(
        grad_in, normed, scale_ref[...], gain_ref[...]
    )


def weight_grad_kernel(core_count, pairs, vectors, place_ref, *refs):
    sides, vector_refs, outs = (
        refs[: 2 * pairs], refs[2 * pairs : 2 * pairs + vectors], refs[2 * pairs + vectors : -2]
    )
    flipped_ref, picked_ref = refs[-2:]
    groups, rows = flipped_ref.shape[0] // core_count, flipped_ref.shape[1]
    jobs = [(sides[2 * at][...], sides[2 * at + 1]) for at in range(pairs)]
    if vectors:
        shape = (LANES, vector_refs[0].shape[1])
        row = lax.broadcasted_iota(jnp.int32, shape, 0)
        stacked = jnp.zeros(shape, f32)
        for at, vector_ref in enumerate(vector_refs):
            stacked = jnp.where(row == at, vector_ref[...], stacked)
        jobs.append((stacked.astype(bf16), None))
    first = 0
    for left, right_ref in jobs:
        flipped_ref[...] = left.T.reshape(flipped_ref.shape)
        width = LANES if right_ref is None else right_ref.shape[1]
        for shift in range(core_count):
            core = lax.rem(place_ref[0] + shift, core_count)
            for group in range(groups):
                picked_ref[group * rows : (group + 1) * rows] = flipped_ref[
                    group * core_count + core
                ]
            part = picked_ref[...]
            if right_ref is not None:
                part = dot_plain(part, right_ref[...]).astype(bf16)
            target = outs[0] if shift == 0 else outs[shift]
            target[:, first : first + width] = part
        first += width


def columns(array, first, width):
    return (array, slice(first, first + width))


def call(kernel, outs, args, scratch=(), scalar=None, flops=0):
    arrays, views = [], []
    for arg in args:
        array, cols = arg if isinstance(arg, tuple) else (arg, None)
        spot = next((k for k, held in enumerate(arrays) if held is array), len(arrays))
        if spot == len(arrays):
            arrays.append(array)
        views.append((spot, cols))
    lead, count = 0 if scalar is None else 1, len(arrays)

    def body(*refs):
        given = refs[lead : lead + count]
        seen = [given[k] if cols is None else given[k].at[:, cols] for k, cols in views]
        kernel(*refs[:lead], *seen, *refs[lead + count :])

    specs = [pl.BlockSpec(memory_space=pltpu.VMEM)] * len(arrays)
    if scalar is not None:
        specs = [pl.BlockSpec(memory_space=pltpu.SMEM), *specs]
        arrays = [scalar, *arrays]
    moved = sum(math.prod(shape) * jnp.dtype(kind).itemsize for shape, kind in outs)
    moved += sum(a.size * a.dtype.itemsize for a in arrays[lead:])

    def run(*operands):
        return pl.pallas_call(
            body,
            out_shape=[jax.ShapeDtypeStruct(shape, kind) for shape, kind in outs],
            in_specs=specs,
            out_specs=[pl.BlockSpec(memory_space=pltpu.VMEM)] * len(outs),
            scratch_shapes=[pltpu.VMEM(shape, kind) for shape, kind in scratch],
            cost_estimate=pl.CostEstimate(flops=flops, bytes_accessed=moved, transcendentals=0),
            compiler_params=pltpu.CompilerParams(vmem_limit_bytes=24 << 20),
        )(*operands)

    return run(*arrays)


def place_kernel(own_ref, held_ref, arrived_ref, out_ref):
    own = own_ref[0]
    out_ref[0, pl.ds(own, 1)] = held_ref[...]
    out_ref[0, pl.ds(1 - own, 1)] = arrived_ref[...]


def place_pair(held, arrived, dim, own):
    outer, width = math.prod(held.shape[:dim]), held.shape[-1]
    rows = math.prod(held.shape[dim:-1])
    block = pl.BlockSpec((1, rows, width), lambda i: (i, 0, 0))
    placed = pl.pallas_call(
        place_kernel,
        grid=(outer,),
        out_shape=jax.ShapeDtypeStruct((outer, 2, rows, width), held.dtype),
        in_specs=[pl.BlockSpec(memory_space=pltpu.SMEM), block, block],
        out_specs=pl.BlockSpec((1, 2, rows, width), lambda i: (i, 0, 0, 0)),
        cost_estimate=pl.CostEstimate(
            flops=0, bytes_accessed=4 * held.size * held.dtype.itemsize, transcendentals=0
        ),
        compiler_params=pltpu.CompilerParams(vmem_limit_bytes=12 << 20),
    )(own.astype(jnp.int32).reshape(1), *(
        cells.reshape(outer, rows, width) for cells in (held, arrived)
    ))
    return placed.reshape(*held.shape[:dim], 2, *held.shape[dim:])


def digits_of(seq_count, shard_count):
    core_count = 2 if seq_count % 2 == 0 else 1
    left = seq_count // core_count
    sizes = []
    while left > 1:
        size = 4 if left % 4 == 0 else 2 if left % 2 == 0 else left
        sizes.append(size)
        left //= size
    digits = []
    stride = seq_count
    for size in (*sizes, core_count):
        stride //= size
        digits.append(("seq", stride, size))
    return (*digits, ("fsdp", 1, shard_count))


def digit_orders(digits):
    core = len(digits) - 2
    near = [core + 1, *reversed(range(core))]
    return (near, [*near[1:2], near[0], *near[2:]])


def own_digit(digit):
    axis, stride, size = digit
    return (lax.axis_index(axis) // stride) % size


def partner(held, shift, size):
    return held ^ shift if size & (size - 1) == 0 else (held + shift) % size


def shift_between(own, place, size):
    return own ^ place if size & (size - 1) == 0 else (own - place) % size


def shift_digit(cells, digit, shift):
    axis, stride, size = digit
    pairs = []
    for index in range(lax.axis_size(axis)):
        held = (index // stride) % size
        pairs.append((index, index + (partner(held, shift, size) - held) * stride))
    return lax.ppermute(cells, axis, pairs)


def take_block(cells, dim, index):
    return lax.dynamic_index_in_dim(cells, index, axis=dim, keepdims=False)


def added(parts):
    total = parts[0].astype(f32)
    for part in parts[1:]:
        total = total + part.astype(f32)
    return total


def blocks_to_send(parts, dim, digit):
    own, size = own_digit(digit), digit[2]
    return [
        added([take_block(part, dim, partner(own, shift, size)) for part in parts]).astype(bf16)
        for shift in range(1, size)
    ]


def sum_digit(parts, blocks, dim, digit):
    own = own_digit(digit)
    arrived = [shift_digit(cells, digit, at + 1) for at, cells in enumerate(blocks)]
    return added([take_block(part, dim, own) for part in parts] + arrived)


def gather_digit(cells, dim, digit):
    size = digit[2]
    own = own_digit(digit)
    arrived = [cells] + [shift_digit(cells, digit, shift) for shift in range(1, size)]
    if size == 2:
        return place_pair(cells, arrived[1], dim, own)
    placed = []
    for place in range(size):
        block = arrived[0]
        for shift in range(1, size):
            block = jnp.where(shift_between(own, place, size) == shift, arrived[shift], block)
        placed.append(block)
    return jnp.stack(placed, axis=dim)


def gather_order(digits, color):
    return [*reversed(digit_orders(digits)[color]), len(digits) - 2]


def gather_rows(shard, color):
    digits = digits_of(lax.axis_size("seq"), lax.axis_size("fsdp"))
    held = []
    for index in gather_order(digits, color):
        dim = sum(other < index for other in held)
        shard = gather_digit(shard, dim, digits[index])
        held.append(index)
    return shard.reshape(-1, shard.shape[-1])


def sum_order(digits, color):
    return [len(digits) - 2, *digit_orders(digits)[color]]


def sum_begin(sent, kept, color):
    digits = digits_of(lax.axis_size("seq"), lax.axis_size("fsdp"))
    core, *near = sum_order(digits, color)
    sizes = [digit[2] for digit in digits]
    parts = [kept] + [
        shift_digit(sent[shift - 1], digits[core], shift)
        for shift in range(1, sizes[core])
    ]
    parts = [part.reshape(*sizes[:core], sizes[-1], -1, part.shape[-1]) for part in parts]
    held = [index for index in range(len(digits)) if index != core]
    return parts, blocks_to_send(parts, held.index(near[0]), digits[near[0]])


def sum_end(parts, blocks, color):
    digits = digits_of(lax.axis_size("seq"), lax.axis_size("fsdp"))
    core, *near = sum_order(digits, color)
    held = [index for index in range(len(digits)) if index != core]
    for stage, index in enumerate(near):
        dim = held.index(index)
        if stage:
            blocks = blocks_to_send(parts, dim, digits[index])
        total = sum_digit(parts, blocks, dim, digits[index])
        parts = [total.astype(bf16)]
        held.remove(index)
    return total


def local(tokens, cotangent, qkv_weight, out_weight, up_weight, down_weight, attn_gain, mlp_gain):
    row_count = tokens.shape[1]
    seq_count = lax.axis_size("seq")
    shard_count = lax.axis_size("fsdp")
    first_row = lax.axis_index("seq") * row_count
    length = row_count * seq_count
    digits = digits_of(seq_count, shard_count)
    core_count = digits[-2][2]
    own_core = own_digit(digits[-2]).astype(jnp.int32).reshape(1)
    place = first_row.astype(jnp.int32).reshape(1)
    grad_factor = 1.0 / math.sqrt(length * shard_count)
    positions = (first_row + jnp.arange(row_count)).astype(f32)
    cosine, sine = rope_tables(positions, HD)
    ends = seq_count - 1
    onward = [(i, i + 1) for i in range(ends)]
    back = [(i + 1, i) for i in range(ends)]

    def halo(cells, pairs):
        return lax.ppermute(cells, "seq", pairs)

    stream = tokens.reshape(row_count, D)
    gains = jnp.concatenate([attn_gain, mlp_gain]).T
    gains = jnp.pad(gains, ((0, 0), (0, LANES - 2 * LAYERS)))
    mixing, widening = [], []
    for n in range(LAYERS):
        packed = [qkv_weight[n], out_weight[n]] + ([gains] if n == 0 else [])
        mixing.append(gather_rows(jnp.concatenate(packed, axis=1), 0))
        packed = jnp.concatenate([up_weight[n], down_weight[n]], axis=1)
        widening.append(gather_rows(packed, 1))
    gains = mixing[0][:, 4 * D : 4 * D + 2 * LAYERS].T
    qkv_all = [columns(array, 0, 3 * D) for array in mixing]
    out_all = [columns(array, 3 * D, D) for array in mixing]
    up_all = [columns(array, 0, 2 * FF) for array in widening]
    down_all = [columns(array, 2 * FF, FF) for array in widening]
    gains_one, gains_two = gains[:LAYERS, None].astype(f32), gains[LAYERS:, None].astype(f32)
    wide = ((row_count, D), f32)
    wide_b = ((row_count, D), bf16)
    column = ((row_count, 1), f32)
    vector = ((1, D), f32)
    edge = ((HALF, 2 * D), bf16)
    lifted_f = ((row_count, FF), f32)
    window = ((row_count + 2 * HALF, 2 * D), bf16)
    unit = 2 * row_count * D
    layer_store = []
    for n in range(LAYERS):
        normed_one, scale_one, attn_in, query, keyval = call(
            project_kernel,
            [wide, column, wide_b, wide_b, ((row_count, 2 * D), bf16)],
            (stream, gains_one[n], qkv_all[n], cosine, sine),
            flops=unit * 3 * D,
        )
        before = halo(keyval[row_count - HALF :], onward)
        after = halo(keyval[:HALF], back)
        (attended, totals, normed_two, scale_two, ffn_in, gate, linear, hidden, stream) = call(
            functools.partial(forward_kernel, length),
            [wide_b, ((row_count, LANES), f32), wide, column, wide_b, lifted_f, lifted_f,
             ((row_count, FF), bf16), wide],
            (query, keyval, before, after, stream, gains_two[n], out_all[n], up_all[n],
             down_all[n]),
            scratch=[window],
            scalar=place,
            flops=unit * (D + 3 * FF),
        )
        layer_store.append(
            (normed_one, scale_one, attn_in, query, keyval, before, after, attended, totals,
             normed_two, scale_two, ffn_in, gate, linear, hidden)
        )
    grad_stream = cotangent.reshape(row_count, D)
    layer_grads = [None] * LAYERS
    sums = []
    chips = D // (seq_count * shard_count) * shard_count

    def weight_grads(sides, vectors=()):
        width = sum(side[1].shape[1] for side in sides) + (LANES if vectors else 0)
        half_rows = D // core_count
        outs = call(
            functools.partial(weight_grad_kernel, core_count, len(sides), len(vectors)),
            [((half_rows, width), bf16)] * core_count,
            [array for side in sides for array in side] + list(vectors),
            scratch=[((D // chips, chips, row_count), bf16), ((half_rows, row_count), bf16)],
            scalar=own_core,
            flops=unit * width,
        )
        return outs[1:], outs[0]

    for n in reversed(range(LAYERS)):
        (normed_one, scale_one, attn_in, query, keyval, before, after, attended, totals,
         normed_two, scale_two, ffn_in, gate, linear, hidden) = layer_store[n]
        (grad_b, grad_lifted, grad_middle, grad_middle_b, gain_two_vec, grad_query, own_grads,
         to_before, to_after) = call(
            functools.partial(backward_kernel, length),
            [wide_b, ((row_count, 2 * FF), bf16), wide, wide_b, vector, wide_b,
             ((row_count, 2 * D), f32), edge, edge],
            (grad_stream, normed_two, scale_two, gate, linear, gains_two[n], down_all[n],
             up_all[n], out_all[n], query, keyval, before, after, totals, cosine, sine),
            scratch=[window, wide],
            scalar=place,
            flops=unit * (D + 3 * FF),
        )
        from_before = halo(to_after, onward)
        from_after = halo(to_before, back)
        outer = weight_grads([(ffn_in, grad_lifted), (grad_b, hidden)])
        grad_projected, grad_stream, gain_one_vec = call(
            input_grad_kernel,
            [((row_count, 3 * D), bf16), wide, vector],
            (grad_query, own_grads, from_before, from_after, qkv_all[n], gains_one[n],
             normed_one, scale_one, grad_middle, cosine, sine),
            scratch=[((row_count, 2 * D), f32)],
            flops=unit * 3 * D,
        )
        inner = weight_grads(
            [(attn_in, grad_projected), (attended, grad_middle_b)], (gain_one_vec, gain_two_vec)
        )
        outer = sum_begin(*outer, 1)
        inner = sum_begin(*inner, 0)
        if n:
            grad_stream, outer, inner = lax.optimization_barrier((grad_stream, outer, inner))
        sums.append((n, outer, inner))
    for n, outer, inner in sums:
        outer = sum_end(*outer, 1)
        inner = sum_end(*inner, 0)
        layer_grads[n] = (
            inner[:, : 3 * D], inner[:, 3 * D : 4 * D], outer[:, : 2 * FF], outer[:, 2 * FF :],
            inner[:, 4 * D], inner[:, 4 * D + 1],
        )
    qkv_part, out_part, up_part, down_part, gain_one_part, gain_two_part = (
        jnp.stack(parts) * grad_factor for parts in zip(*layer_grads)
    )
    return (
        stream.reshape(1, row_count, D),
        grad_stream.reshape(1, row_count, D),
        qkv_part,
        out_part,
        up_part,
        down_part,
        gain_one_part,
        gain_two_part,
    )


def solution(mesh):
    placed = (
        P("fsdp", "seq", None),
        P("fsdp", "seq", None),
        P(None, ("seq", "fsdp"), None),
        P(None, ("seq", "fsdp"), None),
        P(None, ("seq", "fsdp"), None),
        P(None, ("seq", "fsdp"), None),
        P(None, ("seq", "fsdp")),
        P(None, ("seq", "fsdp")),
    )
    return jax.shard_map(
        local,
        mesh=mesh,
        in_specs=placed,
        out_specs=(
            P("fsdp", "seq", None),
            P("fsdp", "seq", None),
            P(None, ("seq", "fsdp"), None),
            P(None, ("seq", "fsdp"), None),
            P(None, ("seq", "fsdp"), None),
            P(None, ("seq", "fsdp"), None),
            P(None, ("seq", "fsdp")),
            P(None, ("seq", "fsdp")),
        ),
        check_vma=False,
    )
```

time: 602 us -> 432 us (0.72)
  waiting for transfers between devices: 388 us -> 230 us
  matrix products: 102 us -> 0 us
  starting transfers between devices: 28.9 us -> 102 us
  Pallas kernels: 0 us -> 62.1 us
  local copies, waits for them, and re-layouts: 36.1 us -> 18.8 us
  other arithmetic: 29.7 us -> 15.7 us
  between operations: 15.3 us -> 1.8 us
    ppermute x8 -> x56, waiting for transfers between devices: 1.15 us -> 230 us  [the longest x48 227 us: shift_digit(): return lax.ppermute(cells, axis, pairs)]
    reduce_scatter x2 -> x0, waiting for transfers between devices: 223 us -> none  [scatter_layer(): lax.psum_scatter(packed, ('seq', 'fsdp'), scatter_dimension=0, tiled=True)]
    all_gather x2 -> x0, waiting for transfers between devices: 164 us -> none  [gather_layer(): whole = lax.all_gather(packed, ('seq', 'fsdp'), axis=0, tiled=True)]
    dot_general x36 -> x0, matrix products: 102 us -> none  [the longest x8 27.7 us: dot_cols(): lax.dot_general(left_side, right_side, (((1,), (1,)), ((), ())), preferre...]
    ppermute x8 -> x56, starting transfers between devices: 28.7 us -> 102 us  [the longest x48 84.7 us: shift_digit(): return lax.ppermute(cells, axis, pairs)]
    pallas_call x0 -> x24, Pallas kernels: none -> 62.1 us  [the longest x12 31.9 us: run(): pl.pallas_call(body, out_shape=[jax.ShapeDtypeStruct(shape, kind) for sha...]
    slice x24 -> x7, local copies, waits for them, and re-layouts: 11.9 us -> 0.43 us  [the longest x2 0.34 us: local(): inner[:, 4 * D + 1]]
    slice x8 -> x0, other arithmetic: 7.14 us -> none  [the longest x4 3.37 us: rotate_back(): values[..., half_size:]]
  transfers between devices with their start and end apart: 12 -> 56, of which waited for: 6 -> 26; matrix products, arithmetic and copies ran while one was open for 10% -> 4% of each run, Pallas kernels for 0% -> 11%
where the time goes in v2:
time: 432 us; the launch traced here: 431 us
  waiting for transfers between devices  230 us (53%)
  starting transfers between devices  102 us (24%)
  Pallas kernels  62.1 us (14%)
  local copies, waits for them, and re-layouts  18.8 us (4%)
  other arithmetic  15.7 us (4%)
    ppermute x48, waiting for transfers between devices, shift_digit(): return lax.ppermute(cells, axis, pairs)  227 us
    ppermute x48, starting transfers between devices, shift_digit(): return lax.ppermute(cells, axis, pairs)  84.7 us
    pallas_call x12, Pallas kernels, run(): pl.pallas_call(body, out_shape=[jax.ShapeDtypeStruct(shape, kind) for sha...  31.9 us
    pallas_call x12, Pallas kernels, place_pair(): pl.pallas_call(place_kernel, grid=(outer,), out_shape=jax.ShapeDtypeStruc...  30.2 us
    ppermute x8, starting transfers between devices, halo(): return lax.ppermute(cells, 'seq', pairs)  17.2 us
    unnamed x73, local copies, waits for them, and re-layouts  13.5 us
  transfers between devices with their start and end apart: 56, of which 26 were waited for; matrix products, arithmetic and copies ran while one was open for 4% of the time, Pallas kernels for 11%

profile of v2, /device:TPU:0, one launch (start us, length us, event | category | flops | bytes accessed | tf_op | source)
XLA Modules:
  0.0 430.7 jit_solution(15081903365017460703)
XLA Ops:
  2.5 5.1 %collective-permute-start.22 = (bf16[24,3456]{1,0:T(8,128)(2,1)S(1)}, bf16[24,3456]{1,0:T(8,128)(2,1)S(1)}, u32[]{:S(2)}, u32[]{:S(2)}) collective-permute-start(bf16[24,3456]{1,0:T(8,128)(2,1)S(1)} %pad_maximum_fusion.5), channel_id=1, source_target_pairs={{0,24},{2,26},{4,28},{6,30},{8,16},{10,18},{12,20},{14,22},{16,8},... | collective-permute-start | bytes 497672 | tf_op jit(solution)/shard_map/ppermute | solution.py:379
  13.4 6.2 %collective-permute-done.14 = bf16[24,3072]{1,0:T(8,128)(2,1)S(1)} collective-permute-done((bf16[24,3072]{1,0:T(8,128)(2,1)S(1)}, bf16[24,3072]{1,0:T(8,128)(2,1)S(1)}, u32[]{:S(2)}, u32[]{:S(2)}) %collective-permute-start.14) | collective-permute-done | bytes 147488 | tf_op jit(solution)/shard_map/ppermute | solution.py:379
  19.6 3.8 collective-permute-start
  23.4 15.2 %collective-permute-done.15 = bf16[24,3072]{1,0:T(8,128)(2,1)S(1)} collective-permute-done((bf16[24,3072]{1,0:T(8,128)(2,1)S(1)}, bf16[24,3072]{1,0:T(8,128)(2,1)S(1)}, u32[]{:S(2)}, u32[]{:S(2)}) %collective-permute-start.15) | collective-permute-done | bytes 147488 | tf_op jit(solution)/shard_map/ppermute | solution.py:379
  38.6 3.2 collective-permute-start.2
  42.2 3.5 collective-permute-start.10
  47.7 2.6 collective-permute-start.8
  52.5 4.2 collective-permute-done.8
  58.2 4.7 %collective-permute-done.9 = bf16[24,3456]{1,0:T(8,128)(2,1)S(1)} collective-permute-done((bf16[24,3456]{1,0:T(8,128)(2,1)S(1)}, bf16[24,3456]{1,0:T(8,128)(2,1)S(1)}, u32[]{:S(2)}, u32[]{:S(2)}) %collective-permute-start.9) | collective-permute-done | bytes 165920 | tf_op jit(solution)/shard_map/ppermute | solution.py:379
  66.6 6.3 %collective-permute-done.17.arrived_ref = bf16[4,24,3072]{2,1,0:T(8,128)(2,1)S(1)} collective-permute-done((bf16[4,24,3072]{2,1,0:T(8,128)(2,1)S(1)}, bf16[4,24,3072]{2,1,0:T(8,128)(2,1)S(1)}, u32[]{:S(2)}, u32[]{:S(2)}) %collective-permute-start.17) | collective-permute-done | bytes 589856 | tf_op jit(solution)/shard_map/ppermute | solution.py:379
  74.6 8.7 %collective-permute-done.3.arrived_ref = bf16[4,24,3200]{2,1,0:T(8,128)(2,1)S(1)} collective-permute-done((bf16[4,24,3200]{2,1,0:T(8,128)(2,1)S(1)}, bf16[4,24,3200]{2,1,0:T(8,128)(2,1)S(1)}, u32[]{:S(2)}, u32[]{:S(2)}) %collective-permute-start.3) | collective-permute-done | bytes 614432 | tf_op jit(solution)/shard_map/ppermute | solution.py:379
  87.6 46.7 %collective-permute-done.4 = bf16[4,2,24,3200]{3,2,1,0:T(8,128)(2,1)S(1)} collective-permute-done((bf16[4,2,24,3200]{3,2,1,0:T(8,128)(2,1)S(1)}, bf16[4,2,24,3200]{3,2,1,0:T(8,128)(2,1)S(1)}, u32[]{:S(2)}, u32[]{:S(2)}) %collective-permute-start.4) | collective-permute-done | bytes 1228832 | tf_op jit(solution)/shard_map/ppermute | solution.py:379
  134.3 3.2 shard_map.144
  137.4 3.1 shard_map.152
  141.0 5.6 %collective-permute-done.25.arrived_ref = bf16[4,24,3456]{2,1,0:T(8,128)(2,1)S(1)} collective-permute-done((bf16[4,24,3456]{2,1,0:T(8,128)(2,1)S(1)}, bf16[4,24,3456]{2,1,0:T(8,128)(2,1)S(1)}, u32[]{:S(2)}, u32[]{:S(2)}) %collective-permute-start.25) | collective-permute-done | bytes 663584 | tf_op jit(solution)/shard_map/ppermute | solution.py:379
  149.4 26.8 %collective-permute-done.26 = bf16[4,2,24,3456]{3,2,1,0:T(8,128)(2,1)S(1)} collective-permute-done((bf16[4,2,24,3456]{3,2,1,0:T(8,128)(2,1)S(1)}, bf16[4,2,24,3456]{3,2,1,0:T(8,128)(2,1)S(1)}, u32[]{:S(2)}, u32[]{:S(2)}) %collective-permute-start.26) | collective-permute-done | bytes 1327136 | tf_op jit(solution)/shard_map/ppermute | solution.py:379
  178.9 4.7 %shard_map.153 = bf16[8,2,48,3072]{3,2,1,0:T(8,128)(2,1)S(1)} custom-call(s32[1]{0:T(128)} %bitcast.2.own_ref.refs_0_, bf16[8,48,3072]{2,1,0:T(8,128)(2,1)} %bitcast.41.held_ref, bf16[8,48,3072]{2,1,0:T(8,128)(2,1)} %bitcast.43.arrived_ref), custom_call_target="tpu_custom_call" | custom-call | bytes 9437184 | tf_op jit(solution)/shard_map/pallas_call | solution.py:322
  185.7 4.8 %shard_map.145 = bf16[8,2,48,3200]{3,2,1,0:T(8,128)(2,1)S(1)} custom-call(s32[1]{0:T(128)} %bitcast.2.own_ref.refs_0_, bf16[8,48,3200]{2,1,0:T(8,128)(2,1)} %bitcast.14.held_ref, bf16[8,48,3200]{2,1,0:T(8,128)(2,1)} %bitcast.16.arrived_ref), custom_call_target="tpu_custom_call" | custom-call | bytes 9830400 | tf_op jit(solution)/shard_map/pallas_call | solution.py:322
  200.7 4.9 %shard_map.149 = bf16[8,2,48,3456]{3,2,1,0:T(8,128)(2,1)S(1)} custom-call(s32[1]{0:T(128)} %bitcast.2.own_ref.refs_0_, bf16[8,48,3456]{2,1,0:T(8,128)(2,1)} %bitcast.29.held_ref, bf16[8,48,3456]{2,1,0:T(8,128)(2,1)} %bitcast.31.arrived_ref), custom_call_target="tpu_custom_call" | custom-call | bytes 10616832 | tf_op jit(solution)/shard_map/pallas_call | solution.py:322
  205.7 2.8 shard_map.150
  211.6 3.0 collective-permute-start.20
  216.2 4.9 %shard_map.157 = bf16[8,2,48,3456]{3,2,1,0:T(8,128)(2,1)S(1)} custom-call(s32[1]{0:T(128)} %bitcast.2.own_ref.refs_0_, bf16[8,48,3456]{2,1,0:T(8,128)(2,1)} %bitcast.53.held_ref, bf16[8,48,3456]{2,1,0:T(8,128)(2,1)} %bitcast.55.arrived_ref), custom_call_target="tpu_custom_call" | custom-call | bytes 10616832 | tf_op jit(solution)/shard_map/pallas_call | solution.py:322
  221.1 3.6 shard_map.158
  224.7 5.2 %shard_map.159 = (bf16[128,768]{1,0:T(8,128)(2,1)S(1)}, bf16[128,2304]{1,0:T(8,128)(2,1)S(1)}, f32[128,768]{1,0:T(8,128)S(1)}, bf16[128,768]{1,0:T(8,128)(2,1)S(...) custom-call(s32[1]{0:T(128)} %bitcast.refs_0_, ...), custom_call_target="tpu_custom_call" | custom-call | flops 830472192 | bytes 16587264 | tf_op jit(solution)/shard_map/pallas_call | solution.py:299
  229.9 3.9 collective-permute-start.28
  235.3 3.0 collective-permute-done.29.refs_3_
  239.7 3.2 shard_map.162
  242.9 4.2 collective-permute-start.31
  247.1 3.2 shard_map.161
  255.4 2.8 collective-permute-done.30
  264.5 5.1 %shard_map.163 = (bf16[128,768]{1,0:T(8,128)(2,1)S(1)}, bf16[128,2304]{1,0:T(8,128)(2,1)S(1)}, f32[128,768]{1,0:T(8,128)S(1)}, bf16[128,768]{1,0:T(8,128)(2,1)S(...) custom-call(s32[1]{0:T(128)} %bitcast.refs_0_, ...), custom_call_target="tpu_custom_call" | custom-call | flops 830472192 | bytes 16783872 | tf_op jit(solution)/shard_map/pallas_call | solution.py:299
  275.0 3.8 collective-permute-start.45
  286.3 3.4 collective-permute-done.40
  291.8 3.2 collective-permute-start.41
  294.9 15.8 %collective-permute-done.51 = bf16[4,2,24,3456]{3,2,0,1:T(8,128)(2,1)S(1)} collective-permute-done((bf16[4,2,24,3456]{3,2,0,1:T(8,128)(2,1)S(1)}, bf16[4,2,24,3456]{3,2,0,1:T(8,128)(2,1)S(1)}, u32[]{:S(2)}, u32[]{:S(2)}) %collective-permute-start.51) | collective-permute-done | bytes 1327136 | tf_op jit(solution)/shard_map/ppermute | solution.py:379
  313.3 10.2 %collective-permute-done.41 = bf16[4,24,3200]{2,1,0:T(8,128)(2,1)S(1)} collective-permute-done((bf16[4,24,3200]{2,1,0:T(8,128)(2,1)S(1)}, bf16[4,24,3200]{2,1,0:T(8,128)(2,1)S(1)}, u32[]{:S(2)}, u32[]{:S(2)}) %collective-permute-start.41) | collective-permute-done | bytes 614432 | tf_op jit(solution)/shard_map/ppermute | solution.py:379
  324.9 3.0 collective-permute-start.43
  328.9 3.3 collective-permute-start.44
  335.3 4.4 %collective-permute-done.44 = bf16[24,3200]{1,0:T(8,128)(2,1)S(1)} collective-permute-done((bf16[24,3200]{1,0:T(8,128)(2,1)S(1)}, bf16[24,3200]{1,0:T(8,128)(2,1)S(1)}, u32[]{:S(2)}, u32[]{:S(2)}) %collective-permute-start.44) | collective-permute-done | bytes 153632 | tf_op jit(solution)/shard_map/ppermute | solution.py:379
  339.7 4.1 collective-permute-start.55
  344.1 8.3 %collective-permute-done.54 = bf16[24,3456]{1,0:T(8,128)(2,1)S(1)} collective-permute-done((bf16[24,3456]{1,0:T(8,128)(2,1)S(1)}, bf16[24,3456]{1,0:T(8,128)(2,1)S(1)}, u32[]{:S(2)}, u32[]{:S(2)}) %collective-permute-start.54) | collective-permute-done | bytes 165920 | tf_op jit(solution)/shard_map/ppermute | solution.py:379
  355.4 25.8 %collective-permute-done.35 = bf16[4,2,24,3200]{3,2,0,1:T(8,128)(2,1)S(1)} collective-permute-done((bf16[4,2,24,3200]{3,2,0,1:T(8,128)(2,1)S(1)}, bf16[4,2,24,3200]{3,2,0,1:T(8,128)(2,1)S(1)}, u32[]{:S(2)}, u32[]{:S(2)}) %collective-permute-start.35) | collective-permute-done | bytes 1228832 | tf_op jit(solution)/shard_map/ppermute | solution.py:379
  382.0 3.7 collective-permute-done.46
  388.5 8.7 %collective-permute-done.36 = bf16[4,24,3200]{2,1,0:T(8,128)(2,1)S(1)} collective-permute-done((bf16[4,24,3200]{2,1,0:T(8,128)(2,1)S(1)}, bf16[4,24,3200]{2,1,0:T(8,128)(2,1)S(1)}, u32[]{:S(2)}, u32[]{:S(2)}) %collective-permute-start.36) | collective-permute-done | bytes 614432 | tf_op jit(solution)/shard_map/ppermute | solution.py:379
  397.5 3.6 collective-permute-start.37
  407.8 2.8 collective-permute-start.50
  410.6 4.1 collective-permute-done.38
  418.2 10.9 %collective-permute-done.49 = bf16[24,3456]{1,0:T(8,128)(2,1)S(1)} collective-permute-done((bf16[24,3456]{1,0:T(8,128)(2,1)S(1)}, bf16[24,3456]{1,0:T(8,128)(2,1)S(1)}, u32[]{:S(2)}, u32[]{:S(2)}) %collective-permute-start.49) | collective-permute-done | bytes 165920 | tf_op jit(solution)/shard_map/ppermute | solution.py:379
  (241 shorter events, 101.4 us)
Async XLA Ops:
  2.5 62.3 %collective-permute-start.22 = (bf16[24,3456]{1,0:T(8,128)(2,1)S(1)}, bf16[24,3456]{1,0:T(8,128)(2,1)S(1)}, u32[]{:S(2)}, u32[]{:S(2)}) collective-permute-start(bf16[24,3456]{1,0:T(8,128)(2,1)S(1)} %pad_maximum_fusion.5), channel_id=1, source_target_pairs={{0,24},{2,26},{4,28},{6,30},{8,16},{10,18},{12,20},{14,22},{16,8},... | collective-permute-start | bytes 497672 | tf_op jit(solution)/shard_map/ppermute | solution.py:379
  7.7 58.7 %collective-permute-start.23 = (bf16[24,3456]{1,0:T(8,128)(2,1)S(1)}, bf16[24,3456]{1,0:T(8,128)(2,1)S(1)}, u32[]{:S(2)}, u32[]{:S(2)}) collective-permute-start(bf16[24,3456]{1,0:T(8,128)(2,1)S(1)} %pad_maximum_fusion.5), channel_id=1, source_target_pairs={{0,16},{2,18},{4,20},{6,22},{8,24},{10,26},{12,28},{14,30},{16,0},... | collective-permute-start | bytes 497672 | tf_op jit(solution)/shard_map/ppermute | solution.py:379
  8.7 10.9 %collective-permute-start.14 = (bf16[24,3072]{1,0:T(8,128)(2,1)S(1)}, bf16[24,3072]{1,0:T(8,128)(2,1)S(1)}, u32[]{:S(2)}, u32[]{:S(2)}) collective-permute-start(bf16[24,3072]{1,0:T(8,128)(2,1)S(1)} %pad_maximum_fusion.6), channel_id=1, source_target_pairs={{0,24},{2,26},{4,28},{6,30},{8,16},{10,18},{12,20},{14,22},{16,8},... | collective-permute-start | bytes 442376 | tf_op jit(solution)/shard_map/ppermute | solution.py:379
  10.7 27.9 %collective-permute-start.15 = (bf16[24,3072]{1,0:T(8,128)(2,1)S(1)}, bf16[24,3072]{1,0:T(8,128)(2,1)S(1)}, u32[]{:S(2)}, u32[]{:S(2)}) collective-permute-start(bf16[24,3072]{1,0:T(8,128)(2,1)S(1)} %pad_maximum_fusion.6), channel_id=1, source_target_pairs={{0,16},{2,18},{4,20},{6,22},{8,24},{10,26},{12,28},{14,30},{16,0},... | collective-permute-start | bytes 442376 | tf_op jit(solution)/shard_map/ppermute | solution.py:379
  11.8 26.9 %collective-permute-start.16 = (bf16[24,3072]{1,0:T(8,128)(2,1)S(1)}, bf16[24,3072]{1,0:T(8,128)(2,1)S(1)}, u32[]{:S(2)}, u32[]{:S(2)}) collective-permute-start(bf16[24,3072]{1,0:T(8,128)(2,1)S(1)} %pad_maximum_fusion.6), channel_id=1, source_target_pairs={{0,8},{2,10},{4,12},{6,14},{8,0},{10,2},{12,4},{14,6},{16,24},{18,... | collective-permute-start | bytes 442376 | tf_op jit(solution)/shard_map/ppermute | solution.py:379
  19.6 22.5 %collective-permute-start = (bf16[24,3200]{1,0:T(8,128)(2,1)S(1)}, bf16[24,3200]{1,0:T(8,128)(2,1)S(1)}, u32[]{:S(2)}, u32[]{:S(2)}) collective-permute-start(bf16[24,3200]{1,0:T(8,128)(2,1)S(1)} %fusion.21), channel_id=1, source_target_pairs={{0,24},{2,26},{4,28},{6,30},{8,16},{10,18},{12,20},{14,22},{16,8},... | collective-permute-start | bytes 460808 | tf_op jit(solution)/shard_map/ppermute | solution.py:379
  38.6 9.0 %collective-permute-start.1 = (bf16[24,3200]{1,0:T(8,128)(2,1)S(1)}, bf16[24,3200]{1,0:T(8,128)(2,1)S(1)}, u32[]{:S(2)}, u32[]{:S(2)}) collective-permute-start(bf16[24,3200]{1,0:T(8,128)(2,1)S(1)} %fusion.21), channel_id=1, source_target_pairs={{0,16},{2,18},{4,20},{6,22},{8,24},{10,26},{12,28},{14,30},{16,0},... | collective-permute-start | bytes 460808 | tf_op jit(solution)/shard_map/ppermute | solution.py:379
  38.6 11.7 %collective-permute-start.2 = (bf16[24,3200]{1,0:T(8,128)(2,1)S(1)}, bf16[24,3200]{1,0:T(8,128)(2,1)S(1)}, u32[]{:S(2)}, u32[]{:S(2)}) collective-permute-start(bf16[24,3200]{1,0:T(8,128)(2,1)S(1)} %fusion.21), channel_id=1, source_target_pairs={{0,8},{2,10},{4,12},{6,14},{8,0},{10,2},{12,4},{14,6},{16,24},{18,... | collective-permute-start | bytes 460808 | tf_op jit(solution)/shard_map/ppermute | solution.py:379
  47.7 9.0 %collective-permute-start.8 = (bf16[24,3456]{1,0:T(8,128)(2,1)S(1)}, bf16[24,3456]{1,0:T(8,128)(2,1)S(1)}, u32[]{:S(2)}, u32[]{:S(2)}) collective-permute-start(bf16[24,3456]{1,0:T(8,128)(2,1)S(1)} %pad_maximum_fusion.4), channel_id=1, source_target_pairs={{0,24},{2,26},{4,28},{6,30},{8,16},{10,18},{12,20},{14,22},{16,8},... | collective-permute-start | bytes 497672 | tf_op jit(solution)/shard_map/ppermute | solution.py:379
  50.3 12.6 %collective-permute-start.9 = (bf16[24,3456]{1,0:T(8,128)(2,1)S(1)}, bf16[24,3456]{1,0:T(8,128)(2,1)S(1)}, u32[]{:S(2)}, u32[]{:S(2)}) collective-permute-start(bf16[24,3456]{1,0:T(8,128)(2,1)S(1)} %pad_maximum_fusion.4), channel_id=1, source_target_pairs={{0,16},{2,18},{4,20},{6,22},{8,24},{10,26},{12,28},{14,30},{16,0},... | collective-permute-start | bytes 497672 | tf_op jit(solution)/shard_map/ppermute | solution.py:379
  50.7 15.7 %collective-permute-start.24 = (bf16[24,3456]{1,0:T(8,128)(2,1)S(1)}, bf16[24,3456]{1,0:T(8,128)(2,1)S(1)}, u32[]{:S(2)}, u32[]{:S(2)}) collective-permute-start(bf16[24,3456]{1,0:T(8,128)(2,1)S(1)} %pad_maximum_fusion.5), channel_id=1, source_target_pairs={{0,8},{2,10},{4,12},{6,14},{8,0},{10,2},{12,4},{14,6},{16,24},{18,... | collective-permute-start | bytes 497672 | tf_op jit(solution)/shard_map/ppermute | solution.py:379
  56.7 16.2 %collective-permute-start.17 = (bf16[4,24,3072]{2,1,0:T(8,128)(2,1)S(1)}, bf16[4,24,3072]{2,1,0:T(8,128)(2,1)S(1)}, u32[]{:S(2)}, u32[]{:S(2)}) collective-permute-start(bf16[4,24,3072]{2,1,0:T(8,128)(2,1)S(1)} %pad_maximum_fusion.3.held_ref), channel_id=1, source_target_pairs={{0,4},{2,6},{4,0},{6,2},{8,12},{10,14},{12,8},{14,10},{16,20},{18,... | collective-permute-start | bytes 1769480 | tf_op jit(solution)/shard_map/ppermute | solution.py:379
  62.9 20.4 %collective-permute-start.3 = (bf16[4,24,3200]{2,1,0:T(8,128)(2,1)S(1)}, bf16[4,24,3200]{2,1,0:T(8,128)(2,1)S(1)}, u32[]{:S(2)}, u32[]{:S(2)}) collective-permute-start(bf16[4,24,3200]{2,1,0:T(8,128)(2,1)S(1)} %pad_maximum_fusion.2.held_ref), channel_id=1, source_target_pairs={{0,4},{2,6},{4,0},{6,2},{8,12},{10,14},{12,8},{14,10},{16,20},{18,... | collective-permute-start | bytes 1843208 | tf_op jit(solution)/shard_map/ppermute | solution.py:379
  64.8 20.2 %collective-permute-start.11 = (bf16[4,24,3456]{2,1,0:T(8,128)(2,1)S(1)}, bf16[4,24,3456]{2,1,0:T(8,128)(2,1)S(1)}, u32[]{:S(2)}, u32[]{:S(2)}) collective-permute-start(bf16[4,24,3456]{2,1,0:T(8,128)(2,1)S(1)} %pad_maximum_fusion.held_ref), channel_id=1, source_target_pairs={{0,1},{1,0},{2,3},{3,2},{4,5},{5,4},{6,7},{7,6},{8,9},{9,8},{10,11... | collective-permute-start | bytes 1990664 | tf_op jit(solution)/shard_map/ppermute | solution.py:379
  73.0 64.4 %collective-permute-start.18 = (bf16[4,2,24,3072]{3,2,1,0:T(8,128)(2,1)S(1)}, bf16[4,2,24,3072]{3,2,1,0:T(8,128)(2,1)S(1)}, u32[]{:S(2)}, u32[]{:S(2)}) collective-permute-start(bf16[4,2,24,3072]{3,2,1,0:T(8,128)(2,1)S(1)} %shard_map.151), channel_id=1, source_target_pairs={{0,1},{1,0},{2,3},{3,2},{4,5},{5,4},{6,7},{7,6},{8,9},{9,8},{10,11... | collective-permute-start | bytes 3538952 | tf_op jit(solution)/shard_map/ppermute | solution.py:379
  83.4 50.9 %collective-permute-start.4 = (bf16[4,2,24,3200]{3,2,1,0:T(8,128)(2,1)S(1)}, bf16[4,2,24,3200]{3,2,1,0:T(8,128)(2,1)S(1)}, u32[]{:S(2)}, u32[]{:S(2)}) collective-permute-start(bf16[4,2,24,3200]{3,2,1,0:T(8,128)(2,1)S(1)} %shard_map.143), channel_id=1, source_target_pairs={{0,1},{1,0},{2,3},{3,2},{4,5},{5,4},{6,7},{7,6},{8,9},{9,8},{10,11... | collective-permute-start | bytes 3686408 | tf_op jit(solution)/shard_map/ppermute | solution.py:379
  85.3 62.2 %collective-permute-start.12 = (bf16[4,2,24,3456]{3,2,1,0:T(8,128)(2,1)S(1)}, bf16[4,2,24,3456]{3,2,1,0:T(8,128)(2,1)S(1)}, u32[]{:S(2)}, u32[]{:S(2)}) collective-permute-start(bf16[4,2,24,3456]{3,2,1,0:T(8,128)(2,1)S(1)} %shard_map.147), channel_id=1, source_target_pairs={{0,4},{2,6},{4,0},{6,2},{8,12},{10,14},{12,8},{14,10},{16,20},{18,... | collective-permute-start | bytes 3981320 | tf_op jit(solution)/shard_map/ppermute | solution.py:379
  87.0 59.7 %collective-permute-start.25 = (bf16[4,24,3456]{2,1,0:T(8,128)(2,1)S(1)}, bf16[4,24,3456]{2,1,0:T(8,128)(2,1)S(1)}, u32[]{:S(2)}, u32[]{:S(2)}) collective-permute-start(bf16[4,24,3456]{2,1,0:T(8,128)(2,1)S(1)} %pad_maximum_fusion.1.held_ref), channel_id=1, source_target_pairs={{0,1},{1,0},{2,3},{3,2},{4,5},{5,4},{6,7},{7,6},{8,9},{9,8},{10,11... | collective-permute-start | bytes 1990664 | tf_op jit(solution)/shard_map/ppermute | solution.py:379
  137.4 48.3 %collective-permute-start.5 = (bf16[4,2,2,24,3200]{4,3,2,1,0:T(8,128)(2,1)}, bf16[4,2,2,24,3200]{4,3,2,1,0:T(8,128)(2,1)}, u32[]{:S(2)}, u32[]{:S(2)}) collective-permute-start(bf16[4,2,2,24,3200]{4,3,2,1,0:T(8,128)(2,1)} %bitcast.15), channel_id=1, source_target_pairs={{0,2},{2,0},{4,6},{6,4},{8,10},{10,8},{12,14},{14,12},{16,18},{18,... | collective-permute-start | bytes 7372808 | tf_op jit(solution)/shard_map/ppermute | solution.py:379
  140.6 38.3 %collective-permute-start.19 = (bf16[4,2,2,24,3072]{4,3,2,1,0:T(8,128)(2,1)}, bf16[4,2,2,24,3072]{4,3,2,1,0:T(8,128)(2,1)}, u32[]{:S(2)}, u32[]{:S(2)}) collective-permute-start(bf16[4,2,2,24,3072]{4,3,2,1,0:T(8,128)(2,1)} %bitcast.42), channel_id=1, source_target_pairs={{0,2},{2,0},{4,6},{6,4},{8,10},{10,8},{12,14},{14,12},{16,18},{18,... | collective-permute-start | bytes 7077896 | tf_op jit(solution)/shard_map/ppermute | solution.py:379
  146.8 29.4 %collective-permute-start.26 = (bf16[4,2,24,3456]{3,2,1,0:T(8,128)(2,1)S(1)}, bf16[4,2,24,3456]{3,2,1,0:T(8,128)(2,1)S(1)}, u32[]{:S(2)}, u32[]{:S(2)}) collective-permute-start(bf16[4,2,24,3456]{3,2,1,0:T(8,128)(2,1)S(1)} %shard_map.155), channel_id=1, source_target_pairs={{0,4},{2,6},{4,0},{6,2},{8,12},{10,14},{12,8},{14,10},{16,20},{18,... | collective-permute-start | bytes 3981320 | tf_op jit(solution)/shard_map/ppermute | solution.py:379
  149.4 51.3 %collective-permute-start.13 = (bf16[4,2,2,24,3456]{4,3,2,1,0:T(8,128)(2,1)}, bf16[4,2,2,24,3456]{4,3,2,1,0:T(8,128)(2,1)}, u32[]{:S(2)}, u32[]{:S(2)}) collective-permute-start(bf16[4,2,2,24,3456]{4,3,2,1,0:T(8,128)(2,1)} %bitcast.30), channel_id=1, source_target_pairs={{0,2},{2,0},{4,6},{6,4},{8,10},{10,8},{12,14},{14,12},{16,18},{18,... | collective-permute-start | bytes 7962632 | tf_op jit(solution)/shard_map/ppermute | solution.py:379
  178.3 37.9 %collective-permute-start.27 = (bf16[4,2,2,24,3456]{4,3,2,1,0:T(8,128)(2,1)}, bf16[4,2,2,24,3456]{4,3,2,1,0:T(8,128)(2,1)}, u32[]{:S(2)}, u32[]{:S(2)}) collective-permute-start(bf16[4,2,2,24,3456]{4,3,2,1,0:T(8,128)(2,1)} %bitcast.54), channel_id=1, source_target_pairs={{0,2},{2,0},{4,6},{6,4},{8,10},{10,8},{12,14},{14,12},{16,18},{18,... | collective-permute-start | bytes 7962632 | tf_op jit(solution)/shard_map/ppermute | solution.py:379
  211.6 9.4 %collective-permute-start.20 = (bf16[64,1536]{1,0:T(8,128)(2,1)S(1)}, bf16[64,1536]{1,0:T(8,128)(2,1)S(1)}, u32[]{:S(2)}, u32[]{:S(2)}) collective-permute-start(bf16[64,1536]{1,0:T(8,128)(2,1)S(1)} %get-tuple-element.180), channel_id=1, source_target_pairs={{0,2},{2,4},{4,6},{6,8},{8,10},{10,12},{12,14},{14,16},{16,18},{18... | collective-permute-start | bytes 589832 | tf_op jit(solution)/shard_map/ppermute | solution.py:485
  242.9 10.4 %collective-permute-start.31 = (bf16[384,3200]{1,0:T(8,128)(2,1)}, bf16[384,3200]{1,0:T(8,128)(2,1)}, u32[]{:S(2)}, u32[]{:S(2)}) collective-permute-start(bf16[384,3200]{1,0:T(8,128)(2,1)} %get-tuple-element.107), channel_id=1, source_target_pairs={{0,2},{2,0},{4,6},{6,4},{8,10},{10,8},{12,14},{14,12},{16,18},{18,... | collective-permute-start | bytes 7372808 | tf_op jit(solution)/shard_map/ppermute | solution.py:379
  260.4 29.4 %collective-permute-start.40 = (bf16[4,2,24,3200]{3,2,0,1:T(8,128)(2,1)S(1)}, bf16[4,2,24,3200]{3,2,0,1:T(8,128)(2,1)S(1)}, u32[]{:S(2)}, u32[]{:S(2)}) collective-permute-start(bf16[4,2,24,3200]{3,2,0,1:T(8,128)(2,1)S(1)} %fusion.8), channel_id=1, source_target_pairs={{0,1},{1,0},{2,3},{3,2},{4,5},{5,4},{6,7},{7,6},{8,9},{9,8},{10,11... | collective-permute-start | bytes 3686408 | tf_op jit(solution)/shard_map/ppermute | solution.py:379
  269.6 11.0 %collective-permute-start.32 = (bf16[64,1536]{1,0:T(8,128)(2,1)S(1)}, bf16[64,1536]{1,0:T(8,128)(2,1)S(1)}, u32[]{:S(2)}, u32[]{:S(2)}) collective-permute-start(bf16[64,1536]{1,0:T(8,128)(2,1)S(1)} %get-tuple-element.116), channel_id=1, source_target_pairs={{0,2},{2,4},{4,6},{6,8},{8,10},{10,12},{12,14},{14,16},{16,18},{18... | collective-permute-start | bytes 589832 | tf_op jit(solution)/shard_map/ppermute | solution.py:485
  271.7 9.0 %collective-permute-start.33 = (bf16[64,1536]{1,0:T(8,128)(2,1)S(1)}, bf16[64,1536]{1,0:T(8,128)(2,1)S(1)}, u32[]{:S(2)}, u32[]{:S(2)}) collective-permute-start(bf16[64,1536]{1,0:T(8,128)(2,1)S(1)} %get-tuple-element.117), channel_id=1, source_target_pairs={{2,0},{4,2},{6,4},{8,6},{10,8},{12,10},{14,12},{16,14},{18,16},{20... | collective-permute-start | bytes 589832 | tf_op jit(solution)/shard_map/ppermute | solution.py:485
  275.0 78.9 %collective-permute-start.45 = (bf16[384,3456]{1,0:T(8,128)(2,1)S(1)}, bf16[384,3456]{1,0:T(8,128)(2,1)S(1)}, u32[]{:S(2)}, u32[]{:S(2)}) collective-permute-start(bf16[384,3456]{1,0:T(8,128)(2,1)S(1)} %get-tuple-element.138), channel_id=1, source_target_pairs={{0,2},{2,0},{4,6},{6,4},{8,10},{10,8},{12,14},{14,12},{16,18},{18,... | collective-permute-start | bytes 7962632 | tf_op jit(solution)/shard_map/ppermute | solution.py:379
  278.7 32.0 %collective-permute-start.51 = (bf16[4,2,24,3456]{3,2,0,1:T(8,128)(2,1)S(1)}, bf16[4,2,24,3456]{3,2,0,1:T(8,128)(2,1)S(1)}, u32[]{:S(2)}, u32[]{:S(2)}) collective-permute-start(bf16[4,2,24,3456]{3,2,0,1:T(8,128)(2,1)S(1)} %fusion.4), channel_id=1, source_target_pairs={{0,4},{2,6},{4,0},{6,2},{8,12},{10,14},{12,8},{14,10},{16,20},{18,... | collective-permute-start | bytes 3981320 | tf_op jit(solution)/shard_map/ppermute | solution.py:379
  284.4 68.1 %collective-permute-start.34 = (bf16[384,3200]{1,0:T(8,128)(2,1)S(1)}, bf16[384,3200]{1,0:T(8,128)(2,1)S(1)}, u32[]{:S(2)}, u32[]{:S(2)}) collective-permute-start(bf16[384,3200]{1,0:T(8,128)(2,1)S(1)} %get-tuple-element.129), channel_id=1, source_target_pairs={{0,2},{2,0},{4,6},{6,4},{8,10},{10,8},{12,14},{14,12},{16,18},{18,... | collective-permute-start | bytes 7372808 | tf_op jit(solution)/shard_map/ppermute | solution.py:379
  291.8 31.7 %collective-permute-start.41 = (bf16[4,24,3200]{2,1,0:T(8,128)(2,1)S(1)}, bf16[4,24,3200]{2,1,0:T(8,128)(2,1)S(1)}, u32[]{:S(2)}, u32[]{:S(2)}) collective-permute-start(bf16[4,24,3200]{2,1,0:T(8,128)(2,1)S(1)} %dynamic-slice_bitcast_fusion.2), channel_id=1, source_target_pairs={{0,4},{2,6},{4,0},{6,2},{8,12},{10,14},{12,8},{14,10},{16,20},{18,... | collective-permute-start | bytes 1843208 | tf_op jit(solution)/shard_map/ppermute | solution.py:379
  312.7 16.2 %collective-permute-start.52 = (bf16[4,24,3456]{2,1,0:T(8,128)(2,1)S(1)}, bf16[4,24,3456]{2,1,0:T(8,128)(2,1)S(1)}, u32[]{:S(2)}, u32[]{:S(2)}) collective-permute-start(bf16[4,24,3456]{2,1,0:T(8,128)(2,1)S(1)} %dynamic-slice_bitcast_fusion), channel_id=1, source_target_pairs={{0,1},{1,0},{2,3},{3,2},{4,5},{5,4},{6,7},{7,6},{8,9},{9,8},{10,11... | collective-permute-start | bytes 1990664 | tf_op jit(solution)/shard_map/ppermute | solution.py:379
  323.7 8.9 %collective-permute-start.42 = (bf16[24,3200]{1,0:T(8,128)(2,1)S(1)}, bf16[24,3200]{1,0:T(8,128)(2,1)S(1)}, u32[]{:S(2)}, u32[]{:S(2)}) collective-permute-start(bf16[24,3200]{1,0:T(8,128)(2,1)S(1)} %get-tuple-element.169), channel_id=1, source_target_pairs={{0,8},{2,10},{4,12},{6,14},{8,0},{10,2},{12,4},{14,6},{16,24},{18,... | collective-permute-start | bytes 460808 | tf_op jit(solution)/shard_map/ppermute | solution.py:379
  328.9 10.8 %collective-permute-start.44 = (bf16[24,3200]{1,0:T(8,128)(2,1)S(1)}, bf16[24,3200]{1,0:T(8,128)(2,1)S(1)}, u32[]{:S(2)}, u32[]{:S(2)}) collective-permute-start(bf16[24,3200]{1,0:T(8,128)(2,1)S(1)} %get-tuple-element.170), channel_id=1, source_target_pairs={{0,24},{2,26},{4,28},{6,30},{8,16},{10,18},{12,20},{14,22},{16,8},... | collective-permute-start | bytes 460808 | tf_op jit(solution)/shard_map/ppermute | solution.py:379
  332.6 11.5 %collective-permute-start.53 = (bf16[24,3456]{1,0:T(8,128)(2,1)S(1)}, bf16[24,3456]{1,0:T(8,128)(2,1)S(1)}, u32[]{:S(2)}, u32[]{:S(2)}) collective-permute-start(bf16[24,3456]{1,0:T(8,128)(2,1)S(1)} %get-tuple-element.157), channel_id=1, source_target_pairs={{0,8},{2,10},{4,12},{6,14},{8,0},{10,2},{12,4},{14,6},{16,24},{18,... | collective-permute-start | bytes 497672 | tf_op jit(solution)/shard_map/ppermute | solution.py:379
  333.0 19.4 %collective-permute-start.54 = (bf16[24,3456]{1,0:T(8,128)(2,1)S(1)}, bf16[24,3456]{1,0:T(8,128)(2,1)S(1)}, u32[]{:S(2)}, u32[]{:S(2)}) collective-permute-start(bf16[24,3456]{1,0:T(8,128)(2,1)S(1)} %get-tuple-element.159), channel_id=1, source_target_pairs={{0,16},{2,18},{4,20},{6,22},{8,24},{10,26},{12,28},{14,30},{16,0},... | collective-permute-start | bytes 497672 | tf_op jit(solution)/shard_map/ppermute | solution.py:379
  339.7 12.8 %collective-permute-start.55 = (bf16[24,3456]{1,0:T(8,128)(2,1)S(1)}, bf16[24,3456]{1,0:T(8,128)(2,1)S(1)}, u32[]{:S(2)}, u32[]{:S(2)}) collective-permute-start(bf16[24,3456]{1,0:T(8,128)(2,1)S(1)} %get-tuple-element.158), channel_id=1, source_target_pairs={{0,24},{2,26},{4,28},{6,30},{8,16},{10,18},{12,20},{14,22},{16,8},... | collective-permute-start | bytes 497672 | tf_op jit(solution)/shard_map/ppermute | solution.py:379
  353.2 27.9 %collective-permute-start.35 = (bf16[4,2,24,3200]{3,2,0,1:T(8,128)(2,1)S(1)}, bf16[4,2,24,3200]{3,2,0,1:T(8,128)(2,1)S(1)}, u32[]{:S(2)}, u32[]{:S(2)}) collective-permute-start(bf16[4,2,24,3200]{3,2,0,1:T(8,128)(2,1)S(1)} %fusion.9), channel_id=1, source_target_pairs={{0,1},{1,0},{2,3},{3,2},{4,5},{5,4},{6,7},{7,6},{8,9},{9,8},{10,11... | collective-permute-start | bytes 3686408 | tf_op jit(solution)/shard_map/ppermute | solution.py:379
  354.3 31.4 %collective-permute-start.46 = (bf16[4,2,24,3456]{3,2,0,1:T(8,128)(2,1)S(1)}, bf16[4,2,24,3456]{3,2,0,1:T(8,128)(2,1)S(1)}, u32[]{:S(2)}, u32[]{:S(2)}) collective-permute-start(bf16[4,2,24,3456]{3,2,0,1:T(8,128)(2,1)S(1)} %fusion.5), channel_id=1, source_target_pairs={{0,4},{2,6},{4,0},{6,2},{8,12},{10,14},{12,8},{14,10},{16,20},{18,... | collective-permute-start | bytes 3981320 | tf_op jit(solution)/shard_map/ppermute | solution.py:379
  381.7 15.6 %collective-permute-start.36 = (bf16[4,24,3200]{2,1,0:T(8,128)(2,1)S(1)}, bf16[4,24,3200]{2,1,0:T(8,128)(2,1)S(1)}, u32[]{:S(2)}, u32[]{:S(2)}) collective-permute-start(bf16[4,24,3200]{2,1,0:T(8,128)(2,1)S(1)} %dynamic-slice_bitcast_fusion.3), channel_id=1, source_target_pairs={{0,4},{2,6},{4,0},{6,2},{8,12},{10,14},{12,8},{14,10},{16,20},{18,... | collective-permute-start | bytes 1843208 | tf_op jit(solution)/shard_map/ppermute | solution.py:379
  386.3 18.2 %collective-permute-start.47 = (bf16[4,24,3456]{2,1,0:T(8,128)(2,1)S(1)}, bf16[4,24,3456]{2,1,0:T(8,128)(2,1)S(1)}, u32[]{:S(2)}, u32[]{:S(2)}) collective-permute-start(bf16[4,24,3456]{2,1,0:T(8,128)(2,1)S(1)} %dynamic-slice_bitcast_fusion.1), channel_id=1, source_target_pairs={{0,1},{1,0},{2,3},{3,2},{4,5},{5,4},{6,7},{7,6},{8,9},{9,8},{10,11... | collective-permute-start | bytes 1990664 | tf_op jit(solution)/shard_map/ppermute | solution.py:379
  397.5 10.3 %collective-permute-start.37 = (bf16[24,3200]{1,0:T(8,128)(2,1)S(1)}, bf16[24,3200]{1,0:T(8,128)(2,1)S(1)}, u32[]{:S(2)}, u32[]{:S(2)}) collective-permute-start(bf16[24,3200]{1,0:T(8,128)(2,1)S(1)} %get-tuple-element.166), channel_id=1, source_target_pairs={{0,8},{2,10},{4,12},{6,14},{8,0},{10,2},{12,4},{14,6},{16,24},{18,... | collective-permute-start | bytes 460808 | tf_op jit(solution)/shard_map/ppermute | solution.py:379
  401.1 13.6 %collective-permute-start.38 = (bf16[24,3200]{1,0:T(8,128)(2,1)S(1)}, bf16[24,3200]{1,0:T(8,128)(2,1)S(1)}, u32[]{:S(2)}, u32[]{:S(2)}) collective-permute-start(bf16[24,3200]{1,0:T(8,128)(2,1)S(1)} %get-tuple-element.168), channel_id=1, source_target_pairs={{0,16},{2,18},{4,20},{6,22},{8,24},{10,26},{12,28},{14,30},{16,0},... | collective-permute-start | bytes 460808 | tf_op jit(solution)/shard_map/ppermute | solution.py:379
  403.1 12.8 %collective-permute-start.39 = (bf16[24,3200]{1,0:T(8,128)(2,1)S(1)}, bf16[24,3200]{1,0:T(8,128)(2,1)S(1)}, u32[]{:S(2)}, u32[]{:S(2)}) collective-permute-start(bf16[24,3200]{1,0:T(8,128)(2,1)S(1)} %get-tuple-element.167), channel_id=1, source_target_pairs={{0,24},{2,26},{4,28},{6,30},{8,16},{10,18},{12,20},{14,22},{16,8},... | collective-permute-start | bytes 460808 | tf_op jit(solution)/shard_map/ppermute | solution.py:379
  404.7 13.5 %collective-permute-start.48 = (bf16[24,3456]{1,0:T(8,128)(2,1)S(1)}, bf16[24,3456]{1,0:T(8,128)(2,1)S(1)}, u32[]{:S(2)}, u32[]{:S(2)}) collective-permute-start(bf16[24,3456]{1,0:T(8,128)(2,1)S(1)} %get-tuple-element.154), channel_id=1, source_target_pairs={{0,8},{2,10},{4,12},{6,14},{8,0},{10,2},{12,4},{14,6},{16,24},{18,... | collective-permute-start | bytes 497672 | tf_op jit(solution)/shard_map/ppermute | solution.py:379
  405.3 23.8 %collective-permute-start.49 = (bf16[24,3456]{1,0:T(8,128)(2,1)S(1)}, bf16[24,3456]{1,0:T(8,128)(2,1)S(1)}, u32[]{:S(2)}, u32[]{:S(2)}) collective-permute-start(bf16[24,3456]{1,0:T(8,128)(2,1)S(1)} %get-tuple-element.156), channel_id=1, source_target_pairs={{0,16},{2,18},{4,20},{6,22},{8,24},{10,26},{12,28},{14,30},{16,0},... | collective-permute-start | bytes 497672 | tf_op jit(solution)/shard_map/ppermute | solution.py:379
  407.8 21.3 %collective-permute-start.50 = (bf16[24,3456]{1,0:T(8,128)(2,1)S(1)}, bf16[24,3456]{1,0:T(8,128)(2,1)S(1)}, u32[]{:S(2)}, u32[]{:S(2)}) collective-permute-start(bf16[24,3456]{1,0:T(8,128)(2,1)S(1)} %get-tuple-element.155), channel_id=1, source_target_pairs={{0,24},{2,26},{4,28},{6,30},{8,16},{10,18},{12,20},{14,22},{16,8},... | collective-permute-start | bytes 497672 | tf_op jit(solution)/shard_map/ppermute | solution.py:379
  (44 other events, 246.9 us)
